TPU v7x, 32 devices: a whole 2x2x4 slice. The times are simulated.
32 devices in a mesh: tp: 4 (over y, core), ad: 8 (over z, x).
Axes of the slice: x: 2, y: 2, z: 4, core: 2. Of those that a mesh axis runs over, the one named last changes fastest.
Arguments:
- hidden: bfloat16 [2048, 8192], P('ad'), may hold values from -6 to 6
- key_value_weight: bfloat16 [8192, 2048], P(None, 'tp'), may hold values from -0.0625 to 0.0625
- request_group: int32 [2048, 1], P('ad'), may hold values from 0 to 7; in each aligned block of 256 rows (0 to 255, 256 to 511, ...) at most 64 rows name the same one
- request_member: int32 [2048], P('ad'), may hold values from 0 to 3
- adapter_down_weight: bfloat16 [8192, 2048], P('tp', 'ad'), may hold values from -0.0625 to 0.0625
- adapter_up_weight: bfloat16 [2048, 2048], P('ad', 'tp'), may hold values from -0.75 to 0.75
Outputs:
- kv_out: bfloat16 [2048, 2048], P('ad', 'tp')
Inputs may be any that keep to these rules, and one draw needn't show every extreme that they name: `request_group`: among the 256 rows of one index of ad, no group is named by more than 64 rows, a bound that some block reaches.
All inputs are finite; a program needn't handle non-finite values.
Results may differ from a plain program's by a relative error of at most 0.007.
Values may be sent and summed in bfloat16 or wider, within the bound.
No kernel may reach another device: no remote copies, remote signals or barrier semaphores. Data moves between devices by JAX's collectives and lax.ppermute only.
A program may use at most 128 MiB of HBM per device.

v0:
```python
import functools

import jax
import jax.numpy as jnp
from jax import lax
from jax.experimental import pallas as pl
from jax.experimental.pallas import tpu as pltpu
from jax.sharding import PartitionSpec as P


ADAPTER_RANK = 64
LANES = 128
LIMIT = pltpu.CompilerParams(vmem_limit_bytes=12 << 20)
IN_HBM = pl.BlockSpec(memory_space=pltpu.HBM)
IN_VMEM = pl.BlockSpec(memory_space=pltpu.VMEM)


def resident(value):
    return pltpu.with_memory_space_constraint(value, pltpu.VMEM)


def stored(value):
    return pltpu.with_memory_space_constraint(value, pltpu.HBM)


def resident_call(kernel, outs):
    def call(*operands):
        return pl.pallas_call(
            kernel,
            in_specs=[IN_VMEM] * len(operands),
            out_specs=[IN_VMEM] * len(outs),
            out_shape=[pltpu.VMEM(*out) for out in outs],
            compiler_params=LIMIT,
        )(*map(resident, operands))

    return call


def pack_kernel(
    n, far, cap, group_hbm, member_hbm, hidden_ref, near_ref, far_ref, *refs
):
    block_refs, (group_ref, member_ref, rows_ref, sems) = refs[:n], refs[n:]
    rows, width = rows_ref.shape
    slots = n * cap
    half = n // 2
    at = pl.multiple_of(lax.axis_index("tp") * width, LANES)
    group_copy = pltpu.make_async_copy(group_hbm, group_ref, sems.at[0])
    member_copy = pltpu.make_async_copy(member_hbm, member_ref, sems.at[1])
    rows_copy = pltpu.make_async_copy(hidden_ref.at[:, pl.ds(at, width)], rows_ref, sems.at[2])
    group_copy.start()
    member_copy.start()
    rows_copy.start()
    group_copy.wait()
    group = group_ref[...]
    by_group = (lax.broadcasted_iota(jnp.int32, (LANES, rows), 0) == group).astype(jnp.float32)
    earlier = (
        lax.broadcasted_iota(jnp.int32, (rows, rows), 0)
        < lax.broadcasted_iota(jnp.int32, (rows, rows), 1)
    ).astype(jnp.bfloat16)
    before = jnp.dot(
        by_group.astype(jnp.bfloat16), earlier, preferred_element_type=jnp.float32
    )
    position = jnp.sum(by_group * before, axis=0, keepdims=True).astype(jnp.int32)
    apart = group ^ lax.axis_index("ad")
    slot = jnp.where(apart < half, apart, half + (apart ^ far)) * cap + position
    chosen = lax.broadcasted_iota(jnp.int32, (slots, rows), 0) == slot
    member_copy.wait()
    code = jnp.sum(
        jnp.where(chosen, member_ref[...].astype(jnp.float32), 0.0), axis=1, keepdims=True
    )
    code = jnp.broadcast_to(code, (slots, LANES)).astype(jnp.bfloat16)
    select = chosen.astype(jnp.bfloat16)
    rows_copy.wait()
    packed = jnp.dot(select, rows_ref[...], preferred_element_type=jnp.float32)
    packed = packed.astype(jnp.bfloat16)
    for k, block_ref in enumerate(block_refs):
        block_ref[:, :width] = packed[k * cap : (k + 1) * cap]
        block_ref[:, width:] = code[k * cap : (k + 1) * cap]
    column = jnp.transpose(jnp.broadcast_to(slot.astype(jnp.float32), (LANES, rows)))[:, :1]
    at_slot = lax.broadcasted_iota(jnp.int32, (rows, half * cap), 1).astype(jnp.float32)
    near_ref[...] = (at_slot == column).astype(jnp.bfloat16)
    far_ref[...] = (at_slot + float(half * cap) == column).astype(jnp.bfloat16)


def pack(group, member, hidden, width, n, far, cap):
    rows = hidden.shape[0]
    spread = pltpu.VMEM((rows, n // 2 * cap), jnp.bfloat16)
    block = pltpu.VMEM((cap, width + LANES), jnp.bfloat16)
    return pl.pallas_call(
        functools.partial(pack_kernel, n, far, cap),
        in_specs=[IN_HBM] * 3,
        out_specs=[IN_VMEM] * (2 + n),
        out_shape=[spread] * 2 + [block] * n,
        scratch_shapes=[
            pltpu.VMEM((1, rows), jnp.int32),
            pltpu.VMEM((1, rows), jnp.int32),
            pltpu.VMEM((rows, width), jnp.bfloat16),
            pltpu.SemaphoreType.DMA((3,)),
        ],
        compiler_params=LIMIT,
        name="pack",
    )(*map(stored, (group, member, hidden)))


def score_kernel(pool, count, *refs):
    block_refs, (down_ref, partial_ref, code_ref) = refs[:count], refs[count:]
    width = down_ref.shape[0]
    rows = jnp.concatenate([ref[:, :width] for ref in block_refs], axis=0)
    code = jnp.concatenate([ref[:, width:] for ref in block_refs], axis=0)
    code_ref[...] = code
    member = code.astype(jnp.float32)
    scores = jnp.dot(rows, down_ref[...], preferred_element_type=jnp.float32)
    total = scores.shape[0]
    upper = lax.broadcasted_iota(jnp.int32, (total, LANES), 1) >= ADAPTER_RANK
    kept = jnp.zeros((total, LANES), jnp.float32)
    for pair in range(pool // 2):
        wanted = jnp.where(upper, 2.0 * pair + 1.0, 2.0 * pair)
        kept = kept + jnp.where(
            member == wanted, scores[:, pair * LANES : (pair + 1) * LANES], 0.0
        )
    both = kept + pltpu.roll(kept, ADAPTER_RANK, 1)
    partial_ref[...] = jnp.where(
        upper[: total // 2], both[total // 2 :], both[: total // 2]
    )


def score(blocks, down, pool):
    total = len(blocks) * blocks[0].shape[0]
    return resident_call(
        functools.partial(score_kernel, pool, len(blocks)),
        [((total // 2, LANES), jnp.float32), ((total, LANES), jnp.bfloat16)],
    )(*blocks, down)


def raise_kernel(pool, count, *refs):
    partial_refs, (code_ref, up_ref), out_refs = refs[:count], refs[count : count + 2], refs[count + 2 :]
    ranks = partial_refs[0][...]
    for ref in partial_refs[1:]:
        ranks = ranks + ref[...]
    lines = ranks.shape[0]
    upper = lax.broadcasted_iota(jnp.int32, (lines, LANES), 1) >= ADAPTER_RANK
    turned = pltpu.roll(ranks, ADAPTER_RANK, 1)
    ranks = jnp.concatenate(
        [jnp.where(upper, turned, ranks), jnp.where(upper, ranks, turned)], axis=0
    )
    member = code_ref[...].astype(jnp.float32)
    upper = lax.broadcasted_iota(jnp.int32, ranks.shape, 1) >= ADAPTER_RANK
    placed = [
        jnp.where(member == jnp.where(upper, 2.0 * pair + 1.0, 2.0 * pair), ranks, 0.0)
        for pair in range(pool // 2)
    ]
    placed = jnp.concatenate(placed, axis=1).astype(jnp.bfloat16)
    raised = jnp.dot(placed, up_ref[...], preferred_element_type=jnp.float32)
    raised = raised.astype(jnp.bfloat16)
    cap = out_refs[0].shape[0]
    for k, ref in enumerate(out_refs):
        ref[...] = raised[k * cap : (k + 1) * cap]


def raise_ranks(partials, code, up, cap, pool):
    outs = code.shape[0] // cap
    return resident_call(
        functools.partial(raise_kernel, pool, len(partials)),
        [((cap, up.shape[1]), jnp.bfloat16)] * outs,
    )(*partials, code, up)


def join_kernel(spread_ref, base_ref, *refs):
    block_refs, out_ref = refs[:-1], refs[-1]
    blocks = jnp.concatenate([ref[...] for ref in block_refs], axis=0)
    update = jnp.dot(spread_ref[...], blocks, preferred_element_type=jnp.float32)
    out_ref[...] = (base_ref[...] + update).astype(out_ref.dtype)


def join(spread, base, blocks, dtype):
    if dtype == jnp.float32:
        return resident_call(join_kernel, [(base.shape, dtype)])(spread, base, *blocks)[0]
    return pl.pallas_call(
        join_kernel,
        in_specs=[IN_VMEM] * (2 + len(blocks)),
        out_shape=jax.ShapeDtypeStruct(base.shape, dtype),
        compiler_params=LIMIT,
    )(*map(resident, (spread, base, *blocks)))


def base_kernel(hidden_ref, weight_ref, out_ref):
    @pl.when(pl.program_id(0) == 0)
    def _():
        out_ref[...] = jnp.zeros_like(out_ref)

    out_ref[...] += jnp.dot(hidden_ref[...], weight_ref[...], preferred_element_type=jnp.float32)


def base_product(hidden, weight, steps):
    (rows, depth), columns = hidden.shape, weight.shape[1]
    step = depth // steps
    return pl.pallas_call(
        base_kernel,
        grid=(steps,),
        in_specs=[
            pl.BlockSpec((rows, step), lambda i: (0, i)),
            pl.BlockSpec((step, columns), lambda i: (i, 0)),
        ],
        out_specs=pl.BlockSpec((rows, columns), lambda i: (0, 0)),
        out_shape=jax.ShapeDtypeStruct((rows, columns), jnp.float32),
        compiler_params=LIMIT,
        name="base_product",
    )(stored(hidden), stored(weight))


def swap(value, axis, size, apart):
    return lax.ppermute(value, axis, [(i, i ^ apart) for i in range(size)])


def shards(
    n_ad, n_tp, hidden, key_value_weight, request_group, request_member, down, up
):
    rows = hidden.shape[0]
    width, pool = down.shape[0], down.shape[1] // ADAPTER_RANK
    cap = 2 * rows // n_ad
    half = n_ad // 2
    far = n_ad - 2 if n_ad > 2 else half
    far_down = swap(down, "ad", n_ad, far)
    near_spread, far_spread, *blocks = pack(
        request_group.reshape(1, rows), request_member.reshape(1, rows), hidden, width, n_ad, far, cap
    )
    near_rows = [blocks[0]] + [swap(blocks[k], "ad", n_ad, k) for k in range(1, half)]
    far_rows = [blocks[half]] + [swap(blocks[half + k], "ad", n_ad, k) for k in range(1, half)]
    base = base_product(hidden, key_value_weight, 4)
    base, *near_rows = lax.optimization_barrier((base, *near_rows))

    def spread_sum(partial):
        return [partial] + [swap(partial, "tp", n_tp, j) for j in range(1, n_tp)]

    def give_back(raised):
        back = [raised[0]]
        for k in range(1, half):
            back.append(swap(raised[k], "ad", n_ad, k))
        return back

    partial, code = score(near_rows, down, pool)
    partial, late_up = lax.optimization_barrier((partial, up))
    far_up = swap(late_up, "ad", n_ad, far)
    raised = raise_ranks(spread_sum(partial), code, up, cap, pool)
    raised, far_rows = lax.optimization_barrier((raised, far_rows))
    base = join(near_spread, base, give_back(raised), jnp.float32)

    partial, code = score(far_rows, far_down, pool)
    raised = raise_ranks(spread_sum(partial), code, far_up, cap, pool)
    return join(far_spread, base, give_back(raised), jnp.bfloat16)


def solution(mesh):
    def step(*arrays):
        return shards(mesh.shape["ad"], mesh.shape["tp"], *arrays)

    placed = (P("ad", None), P(None, "tp"), P("ad", None), P("ad"), P("tp", "ad"), P("ad", "tp"))
    return jax.shard_map(step, mesh=mesh, in_specs=placed, out_specs=P("ad", "tp"), check_vma=False)
```

profile of v0, /device:TPU:0, one launch (start us, length us, event | category | flops | bytes accessed | tf_op | source)
XLA Modules:
  0.0 76.6 jit_solution(9383549687077204697)
XLA Ops:
  0.0 5.1 %collective-permute-start.12 = (bf16[2048,256]{1,0:T(8,128)(2,1)}, bf16[2048,256]{1,0:T(8,128)(2,1)S(1)}, u32[]{:S(2)}, u32[]{:S(2)}) collective-permute-start(bf16[2048,256]{1,0:T(8,128)(2,1)} %refs_4_.1), channel_id=1, source_target_pairs={{0,6},{1,7},{2,4},{3,5},{4,2},{5,3},{6,0},{7,1},{8,14},{9,15},{10,... | collective-permute-start | bytes 3145736 | tf_op jit(solution)/shard_map/ppermute | solution.py:212
  5.1 2.1 %pack.1 = (bf16[256,256]{1,0:T(8,128)(2,1)S(1)}, bf16[256,256]{1,0:T(8,128)(2,1)S(1)}, bf16[64,2176]{1,0:T(8,128)(2,1)S(1)}, bf16[64,2176]{1,0:T(8,128)(2,1)S(1)...) custom-call(s32[1,256]{1,0:T(1,128)} %bitcast.2, ...), custom_call_target="tpu_custom_call" | custom-call | tf_op jit(solution)/shard_map/pack/pallas_call | solution.py:89
  7.2 0.0 copy-start.1
  7.2 1.6 %collective-permute-start = (bf16[64,2176]{1,0:T(8,128)(2,1)S(1)}, bf16[64,2176]{1,0:T(8,128)(2,1)S(1)}, u32[]{:S(2)}, u32[]{:S(2)}) collective-permute-start(bf16[64,2176]{1,0:T(8,128)(2,1)S(1)} %get-tuple-element.45), channel_id=1, source_target_pairs={{0,1},{1,0},{2,3},{3,2},{4,5},{5,4},{6,7},{7,6},{8,9},{9,8},{10,11... | collective-permute-start | bytes 835592 | tf_op jit(solution)/shard_map/ppermute | solution.py:212
  8.8 0.0 collective-permute-start.1
  8.8 2.0 %collective-permute-start.2 = (bf16[64,2176]{1,0:T(8,128)(2,1)S(1)}, bf16[64,2176]{1,0:T(8,128)(2,1)S(1)}, u32[]{:S(2)}, u32[]{:S(2)}) collective-permute-start(bf16[64,2176]{1,0:T(8,128)(2,1)S(1)} %get-tuple-element.47), channel_id=1, source_target_pairs={{0,3},{1,2},{2,1},{3,0},{4,7},{5,6},{6,5},{7,4},{8,11},{9,10},{10,... | collective-permute-start | bytes 835592 | tf_op jit(solution)/shard_map/ppermute | solution.py:212
  10.8 6.5 %base_product.1.base_ref = f32[256,512]{1,0:T(8,128)S(1)} custom-call(bf16[256,8192]{1,0:T(8,128)(2,1)} %hidden_ref.3, bf16[8192,512]{1,0:T(8,128)(2,1)} %weight_ref.1), custom_call_target="tpu_custom_call" | custom-call | tf_op jit(solution)/shard_map/base_product/pallas_call | solution.py:197
  17.2 0.0 collective-permute-done.refs_1_
  17.2 17.6 %collective-permute-done.1.refs_2_ = bf16[64,2176]{1,0:T(8,128)(2,1)S(1)} collective-permute-done((bf16[64,2176]{1,0:T(8,128)(2,1)S(1)}, bf16[64,2176]{1,0:T(8,128)(2,1)S(1)}, u32[]{:S(2)}, u32[]{:S(2)}) %collective-permute-start.1) | collective-permute-done | bytes 278560 | tf_op jit(solution)/shard_map/ppermute | solution.py:212
  34.9 6.6 %collective-permute-done.2.refs_3_ = bf16[64,2176]{1,0:T(8,128)(2,1)S(1)} collective-permute-done((bf16[64,2176]{1,0:T(8,128)(2,1)S(1)}, bf16[64,2176]{1,0:T(8,128)(2,1)S(1)}, u32[]{:S(2)}, u32[]{:S(2)}) %collective-permute-start.2) | collective-permute-done | bytes 278560 | tf_op jit(solution)/shard_map/ppermute | solution.py:212
  41.4 0.5 shard_map.64
  41.9 0.1 collective-permute-start.3
  42.0 1.6 %collective-permute-start.4 = (f32[128,128]{1,0:T(8,128)S(1)}, f32[128,128]{1,0:T(8,128)S(1)}, u32[]{:S(2)}, u32[]{:S(2)}) collective-permute-start(f32[128,128]{1,0:T(8,128)S(1)} %get-tuple-element.54.refs_0_), channel_id=1, source_target_pairs={{0,16},{8,24},{16,0},{24,8},{1,17},{9,25},{17,1},{25,9},{2,18},{10... | collective-permute-start | bytes 196616 | tf_op jit(solution)/shard_map/ppermute | solution.py:212
  43.6 0.5 collective-permute-start.6
  44.1 1.7 %collective-permute-start.7 = (bf16[64,2176]{1,0:T(8,128)(2,1)S(1)}, bf16[64,2176]{1,0:T(8,128)(2,1)S(1)}, u32[]{:S(2)}, u32[]{:S(2)}) collective-permute-start(bf16[64,2176]{1,0:T(8,128)(2,1)S(1)} %get-tuple-element.62), channel_id=1, source_target_pairs={{0,2},{1,3},{2,0},{3,1},{4,6},{5,7},{6,4},{7,5},{8,10},{9,11},{10,... | collective-permute-start | bytes 835592 | tf_op jit(solution)/shard_map/ppermute | solution.py:212
  45.9 0.0 collective-permute-done.3.refs_1_
  45.9 1.2 %collective-permute-start.8 = (bf16[64,2176]{1,0:T(8,128)(2,1)S(1)}, bf16[64,2176]{1,0:T(8,128)(2,1)S(1)}, u32[]{:S(2)}, u32[]{:S(2)}) collective-permute-start(bf16[64,2176]{1,0:T(8,128)(2,1)S(1)} %get-tuple-element.63), channel_id=1, source_target_pairs={{0,3},{1,2},{2,1},{3,0},{4,7},{5,6},{6,5},{7,4},{8,11},{9,10},{10,... | collective-permute-start | bytes 835592 | tf_op jit(solution)/shard_map/ppermute | solution.py:212
  47.1 0.0 collective-permute-done.4.refs_2_
  47.1 0.1 collective-permute-start.5
  47.2 3.8 %collective-permute-done.5.refs_3_ = f32[128,128]{1,0:T(8,128)S(1)} collective-permute-done((f32[128,128]{1,0:T(8,128)S(1)}, f32[128,128]{1,0:T(8,128)S(1)}, u32[]{:S(2)}, u32[]{:S(2)}) %collective-permute-start.5) | collective-permute-done | bytes 65568 | tf_op jit(solution)/shard_map/ppermute | solution.py:212
  51.0 3.5 %collective-permute-start.16 = (bf16[256,512]{1,0:T(8,128)(2,1)S(1)}, bf16[256,512]{1,0:T(8,128)(2,1)S(1)}, u32[]{:S(2)}, u32[]{:S(2)}) collective-permute-start(bf16[256,512]{1,0:T(8,128)(2,1)S(1)} %copy-done.1), channel_id=1, source_target_pairs={{0,6},{1,7},{2,4},{3,5},{4,2},{5,3},{6,0},{7,1},{8,14},{9,15},{10,... | collective-permute-start | bytes 786440 | tf_op jit(solution)/shard_map/ppermute | solution.py:212
  54.5 0.3 shard_map.65
  54.8 0.0 collective-permute-done.6.refs_1_
  54.8 0.0 collective-permute-done.7.refs_2_
  54.8 4.6 %collective-permute-done.8.refs_3_ = bf16[64,2176]{1,0:T(8,128)(2,1)S(1)} collective-permute-done((bf16[64,2176]{1,0:T(8,128)(2,1)S(1)}, bf16[64,2176]{1,0:T(8,128)(2,1)S(1)}, u32[]{:S(2)}, u32[]{:S(2)}) %collective-permute-start.8) | collective-permute-done | bytes 278560 | tf_op jit(solution)/shard_map/ppermute | solution.py:212
  59.5 0.0 collective-permute-done.12.refs_4_
  59.5 0.5 shard_map.67
  60.0 0.1 collective-permute-start.13
  60.1 0.6 collective-permute-start.14
  60.6 1.3 %collective-permute-start.15 = (f32[128,128]{1,0:T(8,128)S(1)}, f32[128,128]{1,0:T(8,128)S(1)}, u32[]{:S(2)}, u32[]{:S(2)}) collective-permute-start(f32[128,128]{1,0:T(8,128)S(1)} %get-tuple-element.72.refs_0_), channel_id=1, source_target_pairs={{0,24},{8,16},{16,8},{24,0},{1,25},{9,17},{17,9},{25,1},{2,26},{10... | collective-permute-start | bytes 196616 | tf_op jit(solution)/shard_map/ppermute | solution.py:212
  61.9 0.9 %collective-permute-start.9 = (bf16[64,512]{1,0:T(8,128)(2,1)S(1)}, bf16[64,512]{1,0:T(8,128)(2,1)S(1)}, u32[]{:S(2)}, u32[]{:S(2)}) collective-permute-start(bf16[64,512]{1,0:T(8,128)(2,1)S(1)} %get-tuple-element.65), channel_id=1, source_target_pairs={{0,1},{1,0},{2,3},{3,2},{4,5},{5,4},{6,7},{7,6},{8,9},{9,8},{10,11... | collective-permute-start | bytes 196616 | tf_op jit(solution)/shard_map/ppermute | solution.py:212
  62.8 3.1 %collective-permute-done.16.refs_5_ = bf16[256,512]{1,0:T(8,128)(2,1)S(1)} collective-permute-done((bf16[256,512]{1,0:T(8,128)(2,1)S(1)}, bf16[256,512]{1,0:T(8,128)(2,1)S(1)}, u32[]{:S(2)}, u32[]{:S(2)}) %collective-permute-start.16) | collective-permute-done | bytes 262176 | tf_op jit(solution)/shard_map/ppermute | solution.py:212
  65.9 0.0 collective-permute-start.10
  65.9 0.0 collective-permute-done.13.refs_1_
  66.0 3.0 %collective-permute-start.11 = (bf16[64,512]{1,0:T(8,128)(2,1)S(1)}, bf16[64,512]{1,0:T(8,128)(2,1)S(1)}, u32[]{:S(2)}, u32[]{:S(2)}) collective-permute-start(bf16[64,512]{1,0:T(8,128)(2,1)S(1)} %get-tuple-element.67), channel_id=1, source_target_pairs={{0,3},{1,2},{2,1},{3,0},{4,7},{5,6},{6,5},{7,4},{8,11},{9,10},{10,... | collective-permute-start | bytes 196616 | tf_op jit(solution)/shard_map/ppermute | solution.py:212
  68.9 0.0 collective-permute-done.14.refs_2_
  68.9 0.0 collective-permute-done.15.refs_3_
  68.9 0.3 shard_map.68
  69.2 0.6 collective-permute-start.17
  69.8 0.0 collective-permute-start.18
  69.8 2.9 %collective-permute-start.19 = (bf16[64,512]{1,0:T(8,128)(2,1)S(1)}, bf16[64,512]{1,0:T(8,128)(2,1)S(1)}, u32[]{:S(2)}, u32[]{:S(2)}) collective-permute-start(bf16[64,512]{1,0:T(8,128)(2,1)S(1)} %get-tuple-element.78), channel_id=1, source_target_pairs={{0,3},{1,2},{2,1},{3,0},{4,7},{5,6},{6,5},{7,4},{8,11},{9,10},{10,... | collective-permute-start | bytes 196616 | tf_op jit(solution)/shard_map/ppermute | solution.py:212
  72.7 0.0 collective-permute-done.10.refs_2_
  72.7 0.0 collective-permute-done.11.refs_3_
  72.8 0.2 shard_map.66.base_ref
  73.0 1.1 %collective-permute-done.17.refs_1_ = bf16[64,512]{1,0:T(8,128)(2,1)S(1)} collective-permute-done((bf16[64,512]{1,0:T(8,128)(2,1)S(1)}, bf16[64,512]{1,0:T(8,128)(2,1)S(1)}, u32[]{:S(2)}, u32[]{:S(2)}) %collective-permute-start.17) | collective-permute-done | bytes 65568 | tf_op jit(solution)/shard_map/ppermute | solution.py:212
  74.1 0.0 collective-permute-done.18.refs_2_
  74.1 1.5 %collective-permute-done.19.refs_3_ = bf16[64,512]{1,0:T(8,128)(2,1)S(1)} collective-permute-done((bf16[64,512]{1,0:T(8,128)(2,1)S(1)}, bf16[64,512]{1,0:T(8,128)(2,1)S(1)}, u32[]{:S(2)}, u32[]{:S(2)}) %collective-permute-start.19) | collective-permute-done | bytes 65568 | tf_op jit(solution)/shard_map/ppermute | solution.py:212
  75.7 0.9 %shard_map.69 = bf16[256,512]{1,0:T(8,128)(2,1)} custom-call(bf16[256,256]{1,0:T(8,128)(2,1)S(1)} %get-tuple-element.42.spread_ref, f32[256,512]{1,0:T(8,128)S(1)} %shard_map.66.base_ref, bf16[64,512]{1,0:T(8,128)(2,1)S(1)} %get-tuple-element.75.refs_0_, bf16[64,512]{1,0:T(8,128)(2,1)S(1)} %collective-permute-done.17.refs_1_, ...), custom_call_target="tpu_custom_call" | custom-call | tf_op jit(solution)/shard_map/pallas_call | solution.py:178
  (4 shorter events, 0.0 us)
Async XLA Ops:
  0.0 59.5 %collective-permute-start.12 = (bf16[2048,256]{1,0:T(8,128)(2,1)}, bf16[2048,256]{1,0:T(8,128)(2,1)S(1)}, u32[]{:S(2)}, u32[]{:S(2)}) collective-permute-start(bf16[2048,256]{1,0:T(8,128)(2,1)} %refs_4_.1), channel_id=1, source_target_pairs={{0,6},{1,7},{2,4},{3,5},{4,2},{5,3},{6,0},{7,1},{8,14},{9,15},{10,... | collective-permute-start | bytes 3145736 | tf_op jit(solution)/shard_map/ppermute | solution.py:212
  5.1 36.3 %copy-start = (bf16[2048,256]{1,0:T(8,128)(2,1)S(1)}, bf16[2048,256]{1,0:T(8,128)(2,1)}, u32[]{:S(2)}) copy-start(bf16[2048,256]{1,0:T(8,128)(2,1)} %refs_4_.1) | copy-start | bytes 3145732
  7.2 43.8 %copy-start.1 = (bf16[256,512]{1,0:T(8,128)(2,1)S(1)}, bf16[256,512]{1,0:T(8,128)(2,1)}, u32[]{:S(2)}) copy-start(bf16[256,512]{1,0:T(8,128)(2,1)} %refs_5_.1) | copy-start | bytes 786436
  7.2 10.0 %collective-permute-start = (bf16[64,2176]{1,0:T(8,128)(2,1)S(1)}, bf16[64,2176]{1,0:T(8,128)(2,1)S(1)}, u32[]{:S(2)}, u32[]{:S(2)}) collective-permute-start(bf16[64,2176]{1,0:T(8,128)(2,1)S(1)} %get-tuple-element.45), channel_id=1, source_target_pairs={{0,1},{1,0},{2,3},{3,2},{4,5},{5,4},{6,7},{7,6},{8,9},{9,8},{10,11... | collective-permute-start | bytes 835592 | tf_op jit(solution)/shard_map/ppermute | solution.py:212
  8.8 26.1 %collective-permute-start.1 = (bf16[64,2176]{1,0:T(8,128)(2,1)S(1)}, bf16[64,2176]{1,0:T(8,128)(2,1)S(1)}, u32[]{:S(2)}, u32[]{:S(2)}) collective-permute-start(bf16[64,2176]{1,0:T(8,128)(2,1)S(1)} %get-tuple-element.46), channel_id=1, source_target_pairs={{0,2},{1,3},{2,0},{3,1},{4,6},{5,7},{6,4},{7,5},{8,10},{9,11},{10,... | collective-permute-start | bytes 835592 | tf_op jit(solution)/shard_map/ppermute | solution.py:212
  8.8 32.6 %collective-permute-start.2 = (bf16[64,2176]{1,0:T(8,128)(2,1)S(1)}, bf16[64,2176]{1,0:T(8,128)(2,1)S(1)}, u32[]{:S(2)}, u32[]{:S(2)}) collective-permute-start(bf16[64,2176]{1,0:T(8,128)(2,1)S(1)} %get-tuple-element.47), channel_id=1, source_target_pairs={{0,3},{1,2},{2,1},{3,0},{4,7},{5,6},{6,5},{7,4},{8,11},{9,10},{10,... | collective-permute-start | bytes 835592 | tf_op jit(solution)/shard_map/ppermute | solution.py:212
  41.9 3.9 %collective-permute-start.3 = (f32[128,128]{1,0:T(8,128)S(1)}, f32[128,128]{1,0:T(8,128)S(1)}, u32[]{:S(2)}, u32[]{:S(2)}) collective-permute-start(f32[128,128]{1,0:T(8,128)S(1)} %get-tuple-element.54.refs_0_), channel_id=1, source_target_pairs={{0,8},{8,0},{16,24},{24,16},{1,9},{9,1},{17,25},{25,17},{2,10},{10... | collective-permute-start | bytes 196616 | tf_op jit(solution)/shard_map/ppermute | solution.py:212
  42.0 5.1 %collective-permute-start.4 = (f32[128,128]{1,0:T(8,128)S(1)}, f32[128,128]{1,0:T(8,128)S(1)}, u32[]{:S(2)}, u32[]{:S(2)}) collective-permute-start(f32[128,128]{1,0:T(8,128)S(1)} %get-tuple-element.54.refs_0_), channel_id=1, source_target_pairs={{0,16},{8,24},{16,0},{24,8},{1,17},{9,25},{17,1},{25,9},{2,18},{10... | collective-permute-start | bytes 196616 | tf_op jit(solution)/shard_map/ppermute | solution.py:212
  43.6 11.2 %collective-permute-start.6 = (bf16[64,2176]{1,0:T(8,128)(2,1)S(1)}, bf16[64,2176]{1,0:T(8,128)(2,1)S(1)}, u32[]{:S(2)}, u32[]{:S(2)}) collective-permute-start(bf16[64,2176]{1,0:T(8,128)(2,1)S(1)} %get-tuple-element.61), channel_id=1, source_target_pairs={{0,1},{1,0},{2,3},{3,2},{4,5},{5,4},{6,7},{7,6},{8,9},{9,8},{10,11... | collective-permute-start | bytes 835592 | tf_op jit(solution)/shard_map/ppermute | solution.py:212
  44.1 10.7 %collective-permute-start.7 = (bf16[64,2176]{1,0:T(8,128)(2,1)S(1)}, bf16[64,2176]{1,0:T(8,128)(2,1)S(1)}, u32[]{:S(2)}, u32[]{:S(2)}) collective-permute-start(bf16[64,2176]{1,0:T(8,128)(2,1)S(1)} %get-tuple-element.62), channel_id=1, source_target_pairs={{0,2},{1,3},{2,0},{3,1},{4,6},{5,7},{6,4},{7,5},{8,10},{9,11},{10,... | collective-permute-start | bytes 835592 | tf_op jit(solution)/shard_map/ppermute | solution.py:212
  45.9 13.6 %collective-permute-start.8 = (bf16[64,2176]{1,0:T(8,128)(2,1)S(1)}, bf16[64,2176]{1,0:T(8,128)(2,1)S(1)}, u32[]{:S(2)}, u32[]{:S(2)}) collective-permute-start(bf16[64,2176]{1,0:T(8,128)(2,1)S(1)} %get-tuple-element.63), channel_id=1, source_target_pairs={{0,3},{1,2},{2,1},{3,0},{4,7},{5,6},{6,5},{7,4},{8,11},{9,10},{10,... | collective-permute-start | bytes 835592 | tf_op jit(solution)/shard_map/ppermute | solution.py:212
  47.1 3.9 %collective-permute-start.5 = (f32[128,128]{1,0:T(8,128)S(1)}, f32[128,128]{1,0:T(8,128)S(1)}, u32[]{:S(2)}, u32[]{:S(2)}) collective-permute-start(f32[128,128]{1,0:T(8,128)S(1)} %get-tuple-element.54.refs_0_), channel_id=1, source_target_pairs={{0,24},{8,16},{16,8},{24,0},{1,25},{9,17},{17,9},{25,1},{2,26},{10... | collective-permute-start | bytes 196616 | tf_op jit(solution)/shard_map/ppermute | solution.py:212
  51.0 15.0 %collective-permute-start.16 = (bf16[256,512]{1,0:T(8,128)(2,1)S(1)}, bf16[256,512]{1,0:T(8,128)(2,1)S(1)}, u32[]{:S(2)}, u32[]{:S(2)}) collective-permute-start(bf16[256,512]{1,0:T(8,128)(2,1)S(1)} %copy-done.1), channel_id=1, source_target_pairs={{0,6},{1,7},{2,4},{3,5},{4,2},{5,3},{6,0},{7,1},{8,14},{9,15},{10,... | collective-permute-start | bytes 786440 | tf_op jit(solution)/shard_map/ppermute | solution.py:212
  60.0 6.0 %collective-permute-start.13 = (f32[128,128]{1,0:T(8,128)S(1)}, f32[128,128]{1,0:T(8,128)S(1)}, u32[]{:S(2)}, u32[]{:S(2)}) collective-permute-start(f32[128,128]{1,0:T(8,128)S(1)} %get-tuple-element.72.refs_0_), channel_id=1, source_target_pairs={{0,8},{8,0},{16,24},{24,16},{1,9},{9,1},{17,25},{25,17},{2,10},{10... | collective-permute-start | bytes 196616 | tf_op jit(solution)/shard_map/ppermute | solution.py:212
  60.1 8.9 %collective-permute-start.14 = (f32[128,128]{1,0:T(8,128)S(1)}, f32[128,128]{1,0:T(8,128)S(1)}, u32[]{:S(2)}, u32[]{:S(2)}) collective-permute-start(f32[128,128]{1,0:T(8,128)S(1)} %get-tuple-element.72.refs_0_), channel_id=1, source_target_pairs={{0,16},{8,24},{16,0},{24,8},{1,17},{9,25},{17,1},{25,9},{2,18},{10... | collective-permute-start | bytes 196616 | tf_op jit(solution)/shard_map/ppermute | solution.py:212
  60.6 8.3 %collective-permute-start.15 = (f32[128,128]{1,0:T(8,128)S(1)}, f32[128,128]{1,0:T(8,128)S(1)}, u32[]{:S(2)}, u32[]{:S(2)}) collective-permute-start(f32[128,128]{1,0:T(8,128)S(1)} %get-tuple-element.72.refs_0_), channel_id=1, source_target_pairs={{0,24},{8,16},{16,8},{24,0},{1,25},{9,17},{17,9},{25,1},{2,26},{10... | collective-permute-start | bytes 196616 | tf_op jit(solution)/shard_map/ppermute | solution.py:212
  61.9 7.9 %collective-permute-start.9 = (bf16[64,512]{1,0:T(8,128)(2,1)S(1)}, bf16[64,512]{1,0:T(8,128)(2,1)S(1)}, u32[]{:S(2)}, u32[]{:S(2)}) collective-permute-start(bf16[64,512]{1,0:T(8,128)(2,1)S(1)} %get-tuple-element.65), channel_id=1, source_target_pairs={{0,1},{1,0},{2,3},{3,2},{4,5},{5,4},{6,7},{7,6},{8,9},{9,8},{10,11... | collective-permute-start | bytes 196616 | tf_op jit(solution)/shard_map/ppermute | solution.py:212
  65.9 6.8 %collective-permute-start.10 = (bf16[64,512]{1,0:T(8,128)(2,1)S(1)}, bf16[64,512]{1,0:T(8,128)(2,1)S(1)}, u32[]{:S(2)}, u32[]{:S(2)}) collective-permute-start(bf16[64,512]{1,0:T(8,128)(2,1)S(1)} %get-tuple-element.66), channel_id=1, source_target_pairs={{0,2},{1,3},{2,0},{3,1},{4,6},{5,7},{6,4},{7,5},{8,10},{9,11},{10,... | collective-permute-start | bytes 196616 | tf_op jit(solution)/shard_map/ppermute | solution.py:212
  66.0 6.8 %collective-permute-start.11 = (bf16[64,512]{1,0:T(8,128)(2,1)S(1)}, bf16[64,512]{1,0:T(8,128)(2,1)S(1)}, u32[]{:S(2)}, u32[]{:S(2)}) collective-permute-start(bf16[64,512]{1,0:T(8,128)(2,1)S(1)} %get-tuple-element.67), channel_id=1, source_target_pairs={{0,3},{1,2},{2,1},{3,0},{4,7},{5,6},{6,5},{7,4},{8,11},{9,10},{10,... | collective-permute-start | bytes 196616 | tf_op jit(solution)/shard_map/ppermute | solution.py:212
  69.2 4.9 %collective-permute-start.17 = (bf16[64,512]{1,0:T(8,128)(2,1)S(1)}, bf16[64,512]{1,0:T(8,128)(2,1)S(1)}, u32[]{:S(2)}, u32[]{:S(2)}) collective-permute-start(bf16[64,512]{1,0:T(8,128)(2,1)S(1)} %get-tuple-element.76), channel_id=1, source_target_pairs={{0,1},{1,0},{2,3},{3,2},{4,5},{5,4},{6,7},{7,6},{8,9},{9,8},{10,11... | collective-permute-start | bytes 196616 | tf_op jit(solution)/shard_map/ppermute | solution.py:212
  69.8 4.4 %collective-permute-start.18 = (bf16[64,512]{1,0:T(8,128)(2,1)S(1)}, bf16[64,512]{1,0:T(8,128)(2,1)S(1)}, u32[]{:S(2)}, u32[]{:S(2)}) collective-permute-start(bf16[64,512]{1,0:T(8,128)(2,1)S(1)} %get-tuple-element.77), channel_id=1, source_target_pairs={{0,2},{1,3},{2,0},{3,1},{4,6},{5,7},{6,4},{7,5},{8,10},{9,11},{10,... | collective-permute-start | bytes 196616 | tf_op jit(solution)/shard_map/ppermute | solution.py:212
  69.8 5.8 %collective-permute-start.19 = (bf16[64,512]{1,0:T(8,128)(2,1)S(1)}, bf16[64,512]{1,0:T(8,128)(2,1)S(1)}, u32[]{:S(2)}, u32[]{:S(2)}) collective-permute-start(bf16[64,512]{1,0:T(8,128)(2,1)S(1)} %get-tuple-element.78), channel_id=1, source_target_pairs={{0,3},{1,2},{2,1},{3,0},{4,7},{5,6},{6,5},{7,4},{8,11},{9,10},{10,... | collective-permute-start | bytes 196616 | tf_op jit(solution)/shard_map/ppermute | solution.py:212
where the time goes:
time: 77.5 us; the launch traced here: 76.6 us
  waiting for transfers between devices  38.4 us (50%)
  starting transfers between devices  26.8 us (35%)
  Pallas kernels  11.3 us (15%)
    ppermute x20, waiting for transfers between devices, swap(): return lax.ppermute(value, axis, [(i, i ^ apart) for i in range(size)])  38.4 us
    ppermute x20, starting transfers between devices, swap(): return lax.ppermute(value, axis, [(i, i ^ apart) for i in range(size)])  26.8 us
    pallas_call x1, Pallas kernels, base_product(): pl.pallas_call(base_kernel, grid=(steps,), in_specs=[pl.BlockSpec((rows,...  6.46 us
    pallas_call x1, Pallas kernels, pack(): pl.pallas_call(functools.partial(pack_kernel, n, far, cap), in_specs=[IN_...  2.11 us
    pallas_call x5, Pallas kernels, call(): pl.pallas_call(kernel, in_specs=[IN_VMEM] * len(operands), out_specs=[IN_...  1.77 us
  transfers between devices with their start and end apart: 20, of which 7 were waited for; matrix products, arithmetic and copies ran while one was open for 0% of the time, Pallas kernels for 14%

commit v1 on v0

--- a/solution.py
+++ b/solution.py
@@ -39,7 +39,8 @@
 def pack_kernel(
     n, far, cap, group_hbm, member_hbm, hidden_ref, near_ref, far_ref, *refs
 ):
-    block_refs, (group_ref, member_ref, rows_ref, sems) = refs[:n], refs[n:]
+    block_refs, code_refs = refs[:n], refs[n : n + n // 2]
+    group_ref, member_ref, rows_ref, sems = refs[n + n // 2 :]
     rows, width = rows_ref.shape
     slots = n * cap
     half = n // 2
@@ -64,18 +65,20 @@
     apart = group ^ lax.axis_index("ad")
     slot = jnp.where(apart < half, apart, half + (apart ^ far)) * cap + position
     chosen = lax.broadcasted_iota(jnp.int32, (slots, rows), 0) == slot
+    select = chosen.astype(jnp.bfloat16)
     member_copy.wait()
-    code = jnp.sum(
-        jnp.where(chosen, member_ref[...].astype(jnp.float32), 0.0), axis=1, keepdims=True
-    )
-    code = jnp.broadcast_to(code, (slots, LANES)).astype(jnp.bfloat16)
-    select = chosen.astype(jnp.bfloat16)
+    member = jnp.broadcast_to(member_ref[...].astype(jnp.float32), (8, rows)).astype(jnp.bfloat16)
+    code = lax.dot_general(
+        member, select, (((1,), (1,)), ((), ())), preferred_element_type=jnp.float32
+    )
     rows_copy.wait()
     packed = jnp.dot(select, rows_ref[...], preferred_element_type=jnp.float32)
     packed = packed.astype(jnp.bfloat16)
     for k, block_ref in enumerate(block_refs):
-        block_ref[:, :width] = packed[k * cap : (k + 1) * cap]
-        block_ref[:, width:] = code[k * cap : (k + 1) * cap]
+        block_ref[...] = packed[k * cap : (k + 1) * cap]
+    for k, code_ref in enumerate(code_refs):
+        code_ref[:, :cap] = code[:, k * cap : (k + 1) * cap]
+        code_ref[:, cap:] = code[:, (half + k) * cap : (half + k + 1) * cap]
     column = jnp.transpose(jnp.broadcast_to(slot.astype(jnp.float32), (LANES, rows)))[:, :1]
     at_slot = lax.broadcasted_iota(jnp.int32, (rows, half * cap), 1).astype(jnp.float32)
     near_ref[...] = (at_slot == column).astype(jnp.bfloat16)
@@ -85,12 +88,13 @@
 def pack(group, member, hidden, width, n, far, cap):
     rows = hidden.shape[0]
     spread = pltpu.VMEM((rows, n // 2 * cap), jnp.bfloat16)
-    block = pltpu.VMEM((cap, width + LANES), jnp.bfloat16)
+    block = pltpu.VMEM((cap, width), jnp.bfloat16)
+    code = pltpu.VMEM((8, 2 * cap), jnp.float32)
     return pl.pallas_call(
         functools.partial(pack_kernel, n, far, cap),
         in_specs=[IN_HBM] * 3,
-        out_specs=[IN_VMEM] * (2 + n),
-        out_shape=[spread] * 2 + [block] * n,
+        out_specs=[IN_VMEM] * (2 + n + n // 2),
+        out_shape=[spread] * 2 + [block] * n + [code] * (n // 2),
         scratch_shapes=[
             pltpu.VMEM((1, rows), jnp.int32),
             pltpu.VMEM((1, rows), jnp.int32),
@@ -102,13 +106,25 @@
     )(*map(stored, (group, member, hidden)))
 
 
+def code_kernel(*refs):
+    code_refs, (near_ref, far_ref) = refs[:-2], refs[-2:]
+    for k, ref in enumerate(code_refs):
+        both = ref.shape[1]
+        columns = jnp.transpose(jnp.broadcast_to(ref[:1, :], (LANES, both)))
+        part = pl.ds(k * (both // 2), both // 2)
+        near_ref[part, :] = columns[: both // 2]
+        far_ref[part, :] = columns[both // 2 :]
+
+
+def spread_codes(codes):
+    total = len(codes) * codes[0].shape[1] // 2
+    return resident_call(code_kernel, [((total, LANES), jnp.float32)] * 2)(*codes)
+
+
 def score_kernel(pool, count, *refs):
-    block_refs, (down_ref, partial_ref, code_ref) = refs[:count], refs[count:]
-    width = down_ref.shape[0]
-    rows = jnp.concatenate([ref[:, :width] for ref in block_refs], axis=0)
-    code = jnp.concatenate([ref[:, width:] for ref in block_refs], axis=0)
-    code_ref[...] = code
-    member = code.astype(jnp.float32)
+    block_refs, (code_ref, down_ref, partial_ref) = refs[:count], refs[count:]
+    rows = jnp.concatenate([ref[...] for ref in block_refs], axis=0)
+    member = code_ref[...]
     scores = jnp.dot(rows, down_ref[...], preferred_element_type=jnp.float32)
     total = scores.shape[0]
     upper = lax.broadcasted_iota(jnp.int32, (total, LANES), 1) >= ADAPTER_RANK
@@ -124,12 +140,11 @@
     )
 
 
-def score(blocks, down, pool):
+def score(blocks, code, down, pool):
     total = len(blocks) * blocks[0].shape[0]
     return resident_call(
-        functools.partial(score_kernel, pool, len(blocks)),
-        [((total // 2, LANES), jnp.float32), ((total, LANES), jnp.bfloat16)],
-    )(*blocks, down)
+        functools.partial(score_kernel, pool, len(blocks)), [((total // 2, LANES), jnp.float32)]
+    )(*blocks, code, down)[0]
 
 
 def raise_kernel(pool, count, *refs):
@@ -143,7 +158,7 @@
     ranks = jnp.concatenate(
         [jnp.where(upper, turned, ranks), jnp.where(upper, ranks, turned)], axis=0
     )
-    member = code_ref[...].astype(jnp.float32)
+    member = code_ref[...]
     upper = lax.broadcasted_iota(jnp.int32, ranks.shape, 1) >= ADAPTER_RANK
     placed = [
         jnp.where(member == jnp.where(upper, 2.0 * pair + 1.0, 2.0 * pair), ranks, 0.0)
@@ -221,11 +236,14 @@
     half = n_ad // 2
     far = n_ad - 2 if n_ad > 2 else half
     far_down = swap(down, "ad", n_ad, far)
-    near_spread, far_spread, *blocks = pack(
+    near_spread, far_spread, *packed = pack(
         request_group.reshape(1, rows), request_member.reshape(1, rows), hidden, width, n_ad, far, cap
     )
+    blocks, codes = packed[:n_ad], packed[n_ad:]
     near_rows = [blocks[0]] + [swap(blocks[k], "ad", n_ad, k) for k in range(1, half)]
     far_rows = [blocks[half]] + [swap(blocks[half + k], "ad", n_ad, k) for k in range(1, half)]
+    codes = [codes[0]] + [swap(codes[k], "ad", n_ad, k) for k in range(1, half)]
+    near_code, far_code = spread_codes(codes)
     base = base_product(hidden, key_value_weight, 4)
     base, *near_rows = lax.optimization_barrier((base, *near_rows))
 
@@ -238,15 +256,14 @@
             back.append(swap(raised[k], "ad", n_ad, k))
         return back
 
-    partial, code = score(near_rows, down, pool)
+    partial = score(near_rows, near_code, down, pool)
     partial, late_up = lax.optimization_barrier((partial, up))
     far_up = swap(late_up, "ad", n_ad, far)
-    raised = raise_ranks(spread_sum(partial), code, up, cap, pool)
-    raised, far_rows = lax.optimization_barrier((raised, far_rows))
+    raised = raise_ranks(spread_sum(partial), near_code, up, cap, pool)
     base = join(near_spread, base, give_back(raised), jnp.float32)
 
-    partial, code = score(far_rows, far_down, pool)
-    raised = raise_ranks(spread_sum(partial), code, far_up, cap, pool)
+    partial = score(far_rows, far_code, far_down, pool)
+    raised = raise_ranks(spread_sum(partial), far_code, far_up, cap, pool)
     return join(far_spread, base, give_back(raised), jnp.bfloat16)
 
 

time: 77.5 us -> 80.2 us (1.035)
  the two profiles are of different devices: /device:TPU:0 before, /device:TPU:16 now
where the time goes in v1:
time: 80.2 us; the launch traced here: 80 us
  waiting for transfers between devices  41.3 us (51%)
  starting transfers between devices  27.2 us (34%)
  Pallas kernels  11.4 us (14%)
    ppermute x23, waiting for transfers between devices, swap(): return lax.ppermute(value, axis, [(i, i ^ apart) for i in range(size)])  41.3 us
    ppermute x23, starting transfers between devices, swap(): return lax.ppermute(value, axis, [(i, i ^ apart) for i in range(size)])  27.2 us
    pallas_call x1, Pallas kernels, base_product(): pl.pallas_call(base_kernel, grid=(steps,), in_specs=[pl.BlockSpec((rows,...  6.46 us
    pallas_call x1, Pallas kernels, pack(): pl.pallas_call(functools.partial(pack_kernel, n, far, cap), in_specs=[IN_...  2.1 us
    pallas_call x6, Pallas kernels, call(): pl.pallas_call(kernel, in_specs=[IN_VMEM] * len(operands), out_specs=[IN_...  1.9 us
  transfers between devices with their start and end apart: 23, of which 8 were waited for; matrix products, arithmetic and copies ran while one was open for 0% of the time, Pallas kernels for 13%

profile of v1, /device:TPU:16, one launch (start us, length us, event | category | flops | bytes accessed | tf_op | source)
XLA Modules:
  0.0 80.0 jit_solution(6798385710569226510)
XLA Ops:
  0.0 0.4 collective-permute-start.15
  0.5 2.1 %pack.1 = (bf16[256,256]{1,0:T(8,128)(2,1)S(1)}, bf16[256,256]{1,0:T(8,128)(2,1)S(1)}, bf16[64,2048]{1,0:T(8,128)(2,1)S(1)}, bf16[64,2048]{1,0:T(8,128)(2,1)S(1)...) custom-call(s32[1,256]{1,0:T(1,128)} %bitcast.2, ...), custom_call_target="tpu_custom_call" | custom-call | tf_op jit(solution)/shard_map/pack/pallas_call | solution.py:93
  2.6 0.0 copy-start.1
  2.6 1.6 %collective-permute-start = (bf16[64,2048]{1,0:T(8,128)(2,1)S(1)}, bf16[64,2048]{1,0:T(8,128)(2,1)S(1)}, u32[]{:S(2)}, u32[]{:S(2)}) collective-permute-start(bf16[64,2048]{1,0:T(8,128)(2,1)S(1)} %get-tuple-element.39), channel_id=1, source_target_pairs={{0,1},{1,0},{2,3},{3,2},{4,5},{5,4},{6,7},{7,6},{8,9},{9,8},{10,11... | collective-permute-start | bytes 786440 | tf_op jit(solution)/shard_map/ppermute | solution.py:227
  4.1 1.3 %collective-permute-start.1 = (bf16[64,2048]{1,0:T(8,128)(2,1)S(1)}, bf16[64,2048]{1,0:T(8,128)(2,1)S(1)}, u32[]{:S(2)}, u32[]{:S(2)}) collective-permute-start(bf16[64,2048]{1,0:T(8,128)(2,1)S(1)} %get-tuple-element.40), channel_id=1, source_target_pairs={{0,2},{1,3},{2,0},{3,1},{4,6},{5,7},{6,4},{7,5},{8,10},{9,11},{10,... | collective-permute-start | bytes 786440 | tf_op jit(solution)/shard_map/ppermute | solution.py:227
  5.5 0.6 collective-permute-start.2
  6.1 1.5 %collective-permute-start.3 = (f32[8,128]{1,0:T(8,128)S(1)}, f32[8,128]{1,0:T(8,128)S(1)}, u32[]{:S(2)}, u32[]{:S(2)}) collective-permute-start(f32[8,128]{1,0:T(8,128)S(1)} %get-tuple-element.48), channel_id=1, source_target_pairs={{0,1},{1,0},{2,3},{3,2},{4,5},{5,4},{6,7},{7,6},{8,9},{9,8},{10,11... | collective-permute-start | bytes 12296 | tf_op jit(solution)/shard_map/ppermute | solution.py:227
  7.6 2.9 %collective-permute-done.3.refs_1_ = f32[8,128]{1,0:T(8,128)S(1)} collective-permute-done((f32[8,128]{1,0:T(8,128)S(1)}, f32[8,128]{1,0:T(8,128)S(1)}, u32[]{:S(2)}, u32[]{:S(2)}) %collective-permute-start.3) | collective-permute-done | bytes 4128 | tf_op jit(solution)/shard_map/ppermute | solution.py:227
  10.5 1.4 %collective-permute-start.4 = (f32[8,128]{1,0:T(8,128)S(1)}, f32[8,128]{1,0:T(8,128)S(1)}, u32[]{:S(2)}, u32[]{:S(2)}) collective-permute-start(f32[8,128]{1,0:T(8,128)S(1)} %get-tuple-element.49), channel_id=1, source_target_pairs={{0,2},{1,3},{2,0},{3,1},{4,6},{5,7},{6,4},{7,5},{8,10},{9,11},{10,... | collective-permute-start | bytes 12296 | tf_op jit(solution)/shard_map/ppermute | solution.py:227
  11.9 25.6 %collective-permute-done.4.refs_2_ = f32[8,128]{1,0:T(8,128)S(1)} collective-permute-done((f32[8,128]{1,0:T(8,128)S(1)}, f32[8,128]{1,0:T(8,128)S(1)}, u32[]{:S(2)}, u32[]{:S(2)}) %collective-permute-start.4) | collective-permute-done | bytes 4128 | tf_op jit(solution)/shard_map/ppermute | solution.py:227
  37.5 3.4 %collective-permute-start.5 = (f32[8,128]{1,0:T(8,128)S(1)}, f32[8,128]{1,0:T(8,128)S(1)}, u32[]{:S(2)}, u32[]{:S(2)}) collective-permute-start(f32[8,128]{1,0:T(8,128)S(1)} %get-tuple-element.50), channel_id=1, source_target_pairs={{0,3},{1,2},{2,1},{3,0},{4,7},{5,6},{6,5},{7,4},{8,11},{9,10},{10,... | collective-permute-start | bytes 12296 | tf_op jit(solution)/shard_map/ppermute | solution.py:227
  40.8 1.6 %collective-permute-done.5.refs_3_ = f32[8,128]{1,0:T(8,128)S(1)} collective-permute-done((f32[8,128]{1,0:T(8,128)S(1)}, f32[8,128]{1,0:T(8,128)S(1)}, u32[]{:S(2)}, u32[]{:S(2)}) %collective-permute-start.5) | collective-permute-done | bytes 4128 | tf_op jit(solution)/shard_map/ppermute | solution.py:227
  42.4 1.0 %collective-permute-start.12 = (bf16[64,2048]{1,0:T(8,128)(2,1)S(1)}, bf16[64,2048]{1,0:T(8,128)(2,1)S(1)}, u32[]{:S(2)}, u32[]{:S(2)}) collective-permute-start(bf16[64,2048]{1,0:T(8,128)(2,1)S(1)} %get-tuple-element.58), channel_id=1, source_target_pairs={{0,1},{1,0},{2,3},{3,2},{4,5},{5,4},{6,7},{7,6},{8,9},{9,8},{10,11... | collective-permute-start | bytes 786440 | tf_op jit(solution)/shard_map/ppermute | solution.py:227
  43.5 0.0 collective-permute-done.refs_1_
  43.5 2.5 %collective-permute-start.13 = (bf16[64,2048]{1,0:T(8,128)(2,1)S(1)}, bf16[64,2048]{1,0:T(8,128)(2,1)S(1)}, u32[]{:S(2)}, u32[]{:S(2)}) collective-permute-start(bf16[64,2048]{1,0:T(8,128)(2,1)S(1)} %get-tuple-element.59), channel_id=1, source_target_pairs={{0,2},{1,3},{2,0},{3,1},{4,6},{5,7},{6,4},{7,5},{8,10},{9,11},{10,... | collective-permute-start | bytes 786440 | tf_op jit(solution)/shard_map/ppermute | solution.py:227
  45.9 0.0 collective-permute-done.1.refs_2_
  45.9 0.0 collective-permute-start.14
  46.0 6.5 %base_product.1.base_ref = f32[256,512]{1,0:T(8,128)S(1)} custom-call(bf16[256,8192]{1,0:T(8,128)(2,1)} %hidden_ref.3, bf16[8192,512]{1,0:T(8,128)(2,1)} %weight_ref.1), custom_call_target="tpu_custom_call" | custom-call | tf_op jit(solution)/shard_map/base_product/pallas_call | solution.py:212
  52.4 0.1 shard_map.64
  52.6 0.0 collective-permute-done.2.refs_3_
  52.6 0.5 shard_map.65.refs_0_
  53.1 1.1 %collective-permute-start.19 = (bf16[256,512]{1,0:T(8,128)(2,1)S(1)}, bf16[256,512]{1,0:T(8,128)(2,1)S(1)}, u32[]{:S(2)}, u32[]{:S(2)}) collective-permute-start(bf16[256,512]{1,0:T(8,128)(2,1)S(1)} %copy-done.1), channel_id=1, source_target_pairs={{0,6},{1,7},{2,4},{3,5},{4,2},{5,3},{6,0},{7,1},{8,14},{9,15},{10,... | collective-permute-start | bytes 786440 | tf_op jit(solution)/shard_map/ppermute | solution.py:227
  54.2 0.0 collective-permute-done.12.refs_1_
  54.2 0.0 collective-permute-start.6
  54.2 1.6 %collective-permute-start.7 = (f32[128,128]{1,0:T(8,128)S(1)}, f32[128,128]{1,0:T(8,128)S(1)}, u32[]{:S(2)}, u32[]{:S(2)}) collective-permute-start(f32[128,128]{1,0:T(8,128)S(1)} %shard_map.65.refs_0_), channel_id=1, source_target_pairs={{0,16},{8,24},{16,0},{24,8},{1,17},{9,25},{17,1},{25,9},{2,18},{10... | collective-permute-start | bytes 196616 | tf_op jit(solution)/shard_map/ppermute | solution.py:227
  55.8 5.6 %collective-permute-done.14.refs_3_ = bf16[64,2048]{1,0:T(8,128)(2,1)S(1)} collective-permute-done((bf16[64,2048]{1,0:T(8,128)(2,1)S(1)}, bf16[64,2048]{1,0:T(8,128)(2,1)S(1)}, u32[]{:S(2)}, u32[]{:S(2)}) %collective-permute-start.14) | collective-permute-done | bytes 262176 | tf_op jit(solution)/shard_map/ppermute | solution.py:227
  61.5 0.0 collective-permute-start.8
  61.5 0.0 collective-permute-done.15.refs_5_
  61.5 0.5 shard_map.68.refs_0_
  62.0 1.7 %collective-permute-start.16 = (f32[128,128]{1,0:T(8,128)S(1)}, f32[128,128]{1,0:T(8,128)S(1)}, u32[]{:S(2)}, u32[]{:S(2)}) collective-permute-start(f32[128,128]{1,0:T(8,128)S(1)} %shard_map.68.refs_0_), channel_id=1, source_target_pairs={{0,8},{8,0},{16,24},{24,16},{1,9},{9,1},{17,25},{25,17},{2,10},{10... | collective-permute-start | bytes 196616 | tf_op jit(solution)/shard_map/ppermute | solution.py:227
  63.7 0.0 collective-permute-done.6.refs_1_
  63.7 0.5 collective-permute-start.17
  64.2 0.0 collective-permute-done.7.refs_2_
  64.2 0.9 %collective-permute-start.18 = (f32[128,128]{1,0:T(8,128)S(1)}, f32[128,128]{1,0:T(8,128)S(1)}, u32[]{:S(2)}, u32[]{:S(2)}) collective-permute-start(f32[128,128]{1,0:T(8,128)S(1)} %shard_map.68.refs_0_), channel_id=1, source_target_pairs={{0,24},{8,16},{16,8},{24,0},{1,25},{9,17},{17,9},{25,1},{2,26},{10... | collective-permute-start | bytes 196616 | tf_op jit(solution)/shard_map/ppermute | solution.py:227
  65.1 0.7 collective-permute-done.8.refs_3_
  65.8 0.3 shard_map.66
  66.1 0.1 collective-permute-start.9
  66.1 3.9 %collective-permute-start.10 = (bf16[64,512]{1,0:T(8,128)(2,1)S(1)}, bf16[64,512]{1,0:T(8,128)(2,1)S(1)}, u32[]{:S(2)}, u32[]{:S(2)}) collective-permute-start(bf16[64,512]{1,0:T(8,128)(2,1)S(1)} %get-tuple-element.55), channel_id=1, source_target_pairs={{0,2},{1,3},{2,0},{3,1},{4,6},{5,7},{6,4},{7,5},{8,10},{9,11},{10,... | collective-permute-start | bytes 196616 | tf_op jit(solution)/shard_map/ppermute | solution.py:227
  70.1 0.0 collective-permute-done.18.refs_3_
  70.1 0.3 shard_map.69
  70.4 1.6 %collective-permute-start.20 = (bf16[64,512]{1,0:T(8,128)(2,1)S(1)}, bf16[64,512]{1,0:T(8,128)(2,1)S(1)}, u32[]{:S(2)}, u32[]{:S(2)}) collective-permute-start(bf16[64,512]{1,0:T(8,128)(2,1)S(1)} %get-tuple-element.64), channel_id=1, source_target_pairs={{0,1},{1,0},{2,3},{3,2},{4,5},{5,4},{6,7},{7,6},{8,9},{9,8},{10,11... | collective-permute-start | bytes 196616 | tf_op jit(solution)/shard_map/ppermute | solution.py:227
  72.0 2.0 %collective-permute-start.21 = (bf16[64,512]{1,0:T(8,128)(2,1)S(1)}, bf16[64,512]{1,0:T(8,128)(2,1)S(1)}, u32[]{:S(2)}, u32[]{:S(2)}) collective-permute-start(bf16[64,512]{1,0:T(8,128)(2,1)S(1)} %get-tuple-element.65), channel_id=1, source_target_pairs={{0,2},{1,3},{2,0},{3,1},{4,6},{5,7},{6,4},{7,5},{8,10},{9,11},{10,... | collective-permute-start | bytes 196616 | tf_op jit(solution)/shard_map/ppermute | solution.py:227
  73.9 0.0 collective-permute-start.22
  73.9 1.4 %collective-permute-done.11.refs_3_ = bf16[64,512]{1,0:T(8,128)(2,1)S(1)} collective-permute-done((bf16[64,512]{1,0:T(8,128)(2,1)S(1)}, bf16[64,512]{1,0:T(8,128)(2,1)S(1)}, u32[]{:S(2)}, u32[]{:S(2)}) %collective-permute-start.11) | collective-permute-done | bytes 65568 | tf_op jit(solution)/shard_map/ppermute | solution.py:227
  75.3 0.2 shard_map.67.base_ref
  75.6 1.1 %collective-permute-done.21.refs_2_ = bf16[64,512]{1,0:T(8,128)(2,1)S(1)} collective-permute-done((bf16[64,512]{1,0:T(8,128)(2,1)S(1)}, bf16[64,512]{1,0:T(8,128)(2,1)S(1)}, u32[]{:S(2)}, u32[]{:S(2)}) %collective-permute-start.21) | collective-permute-done | bytes 65568 | tf_op jit(solution)/shard_map/ppermute | solution.py:227
  76.6 2.4 %collective-permute-done.22.refs_3_ = bf16[64,512]{1,0:T(8,128)(2,1)S(1)} collective-permute-done((bf16[64,512]{1,0:T(8,128)(2,1)S(1)}, bf16[64,512]{1,0:T(8,128)(2,1)S(1)}, u32[]{:S(2)}, u32[]{:S(2)}) %collective-permute-start.22) | collective-permute-done | bytes 65568 | tf_op jit(solution)/shard_map/ppermute | solution.py:227
  79.1 0.9 %shard_map.70 = bf16[256,512]{1,0:T(8,128)(2,1)} custom-call(bf16[256,256]{1,0:T(8,128)(2,1)S(1)} %get-tuple-element.36.spread_ref, f32[256,512]{1,0:T(8,128)S(1)} %shard_map.67.base_ref, bf16[64,512]{1,0:T(8,128)(2,1)S(1)} %get-tuple-element.63.refs_0_, bf16[64,512]{1,0:T(8,128)(2,1)S(1)} %collective-permute-done.20.refs_1_, ...), custom_call_target="tpu_custom_call" | custom-call | tf_op jit(solution)/shard_map/pallas_call | solution.py:193
  (11 shorter events, 0.0 us)
Async XLA Ops:
  0.0 61.5 %collective-permute-start.15 = (bf16[2048,256]{1,0:T(8,128)(2,1)}, bf16[2048,256]{1,0:T(8,128)(2,1)S(1)}, u32[]{:S(2)}, u32[]{:S(2)}) collective-permute-start(bf16[2048,256]{1,0:T(8,128)(2,1)} %refs_5_.2), channel_id=1, source_target_pairs={{0,6},{1,7},{2,4},{3,5},{4,2},{5,3},{6,0},{7,1},{8,14},{9,15},{10,... | collective-permute-start | bytes 3145736 | tf_op jit(solution)/shard_map/ppermute | solution.py:227
  0.5 52.1 %copy-start = (bf16[2048,256]{1,0:T(8,128)(2,1)S(1)}, bf16[2048,256]{1,0:T(8,128)(2,1)}, u32[]{:S(2)}) copy-start(bf16[2048,256]{1,0:T(8,128)(2,1)} %refs_5_.2) | copy-start | bytes 3145732
  2.6 50.5 %copy-start.1 = (bf16[256,512]{1,0:T(8,128)(2,1)S(1)}, bf16[256,512]{1,0:T(8,128)(2,1)}, u32[]{:S(2)}) copy-start(bf16[256,512]{1,0:T(8,128)(2,1)} %refs_5_.3) | copy-start | bytes 786436
  2.6 40.9 %collective-permute-start = (bf16[64,2048]{1,0:T(8,128)(2,1)S(1)}, bf16[64,2048]{1,0:T(8,128)(2,1)S(1)}, u32[]{:S(2)}, u32[]{:S(2)}) collective-permute-start(bf16[64,2048]{1,0:T(8,128)(2,1)S(1)} %get-tuple-element.39), channel_id=1, source_target_pairs={{0,1},{1,0},{2,3},{3,2},{4,5},{5,4},{6,7},{7,6},{8,9},{9,8},{10,11... | collective-permute-start | bytes 786440 | tf_op jit(solution)/shard_map/ppermute | solution.py:227
  4.1 41.8 %collective-permute-start.1 = (bf16[64,2048]{1,0:T(8,128)(2,1)S(1)}, bf16[64,2048]{1,0:T(8,128)(2,1)S(1)}, u32[]{:S(2)}, u32[]{:S(2)}) collective-permute-start(bf16[64,2048]{1,0:T(8,128)(2,1)S(1)} %get-tuple-element.40), channel_id=1, source_target_pairs={{0,2},{1,3},{2,0},{3,1},{4,6},{5,7},{6,4},{7,5},{8,10},{9,11},{10,... | collective-permute-start | bytes 786440 | tf_op jit(solution)/shard_map/ppermute | solution.py:227
  5.5 47.1 %collective-permute-start.2 = (bf16[64,2048]{1,0:T(8,128)(2,1)S(1)}, bf16[64,2048]{1,0:T(8,128)(2,1)S(1)}, u32[]{:S(2)}, u32[]{:S(2)}) collective-permute-start(bf16[64,2048]{1,0:T(8,128)(2,1)S(1)} %get-tuple-element.41), channel_id=1, source_target_pairs={{0,3},{1,2},{2,1},{3,0},{4,7},{5,6},{6,5},{7,4},{8,11},{9,10},{10,... | collective-permute-start | bytes 786440 | tf_op jit(solution)/shard_map/ppermute | solution.py:227
  6.1 4.4 %collective-permute-start.3 = (f32[8,128]{1,0:T(8,128)S(1)}, f32[8,128]{1,0:T(8,128)S(1)}, u32[]{:S(2)}, u32[]{:S(2)}) collective-permute-start(f32[8,128]{1,0:T(8,128)S(1)} %get-tuple-element.48), channel_id=1, source_target_pairs={{0,1},{1,0},{2,3},{3,2},{4,5},{5,4},{6,7},{7,6},{8,9},{9,8},{10,11... | collective-permute-start | bytes 12296 | tf_op jit(solution)/shard_map/ppermute | solution.py:227
  10.5 27.0 %collective-permute-start.4 = (f32[8,128]{1,0:T(8,128)S(1)}, f32[8,128]{1,0:T(8,128)S(1)}, u32[]{:S(2)}, u32[]{:S(2)}) collective-permute-start(f32[8,128]{1,0:T(8,128)S(1)} %get-tuple-element.49), channel_id=1, source_target_pairs={{0,2},{1,3},{2,0},{3,1},{4,6},{5,7},{6,4},{7,5},{8,10},{9,11},{10,... | collective-permute-start | bytes 12296 | tf_op jit(solution)/shard_map/ppermute | solution.py:227
  37.5 5.0 %collective-permute-start.5 = (f32[8,128]{1,0:T(8,128)S(1)}, f32[8,128]{1,0:T(8,128)S(1)}, u32[]{:S(2)}, u32[]{:S(2)}) collective-permute-start(f32[8,128]{1,0:T(8,128)S(1)} %get-tuple-element.50), channel_id=1, source_target_pairs={{0,3},{1,2},{2,1},{3,0},{4,7},{5,6},{6,5},{7,4},{8,11},{9,10},{10,... | collective-permute-start | bytes 12296 | tf_op jit(solution)/shard_map/ppermute | solution.py:227
  42.4 11.8 %collective-permute-start.12 = (bf16[64,2048]{1,0:T(8,128)(2,1)S(1)}, bf16[64,2048]{1,0:T(8,128)(2,1)S(1)}, u32[]{:S(2)}, u32[]{:S(2)}) collective-permute-start(bf16[64,2048]{1,0:T(8,128)(2,1)S(1)} %get-tuple-element.58), channel_id=1, source_target_pairs={{0,1},{1,0},{2,3},{3,2},{4,5},{5,4},{6,7},{7,6},{8,9},{9,8},{10,11... | collective-permute-start | bytes 786440 | tf_op jit(solution)/shard_map/ppermute | solution.py:227
  43.5 10.8 %collective-permute-start.13 = (bf16[64,2048]{1,0:T(8,128)(2,1)S(1)}, bf16[64,2048]{1,0:T(8,128)(2,1)S(1)}, u32[]{:S(2)}, u32[]{:S(2)}) collective-permute-start(bf16[64,2048]{1,0:T(8,128)(2,1)S(1)} %get-tuple-element.59), channel_id=1, source_target_pairs={{0,2},{1,3},{2,0},{3,1},{4,6},{5,7},{6,4},{7,5},{8,10},{9,11},{10,... | collective-permute-start | bytes 786440 | tf_op jit(solution)/shard_map/ppermute | solution.py:227
  45.9 15.5 %collective-permute-start.14 = (bf16[64,2048]{1,0:T(8,128)(2,1)S(1)}, bf16[64,2048]{1,0:T(8,128)(2,1)S(1)}, u32[]{:S(2)}, u32[]{:S(2)}) collective-permute-start(bf16[64,2048]{1,0:T(8,128)(2,1)S(1)} %get-tuple-element.60), channel_id=1, source_target_pairs={{0,3},{1,2},{2,1},{3,0},{4,7},{5,6},{6,5},{7,4},{8,11},{9,10},{10,... | collective-permute-start | bytes 786440 | tf_op jit(solution)/shard_map/ppermute | solution.py:227
  53.1 13.0 %collective-permute-start.19 = (bf16[256,512]{1,0:T(8,128)(2,1)S(1)}, bf16[256,512]{1,0:T(8,128)(2,1)S(1)}, u32[]{:S(2)}, u32[]{:S(2)}) collective-permute-start(bf16[256,512]{1,0:T(8,128)(2,1)S(1)} %copy-done.1), channel_id=1, source_target_pairs={{0,6},{1,7},{2,4},{3,5},{4,2},{5,3},{6,0},{7,1},{8,14},{9,15},{10,... | collective-permute-start | bytes 786440 | tf_op jit(solution)/shard_map/ppermute | solution.py:227
  54.2 9.5 %collective-permute-start.6 = (f32[128,128]{1,0:T(8,128)S(1)}, f32[128,128]{1,0:T(8,128)S(1)}, u32[]{:S(2)}, u32[]{:S(2)}) collective-permute-start(f32[128,128]{1,0:T(8,128)S(1)} %shard_map.65.refs_0_), channel_id=1, source_target_pairs={{0,8},{8,0},{16,24},{24,16},{1,9},{9,1},{17,25},{25,17},{2,10},{10... | collective-permute-start | bytes 196616 | tf_op jit(solution)/shard_map/ppermute | solution.py:227
  54.2 10.0 %collective-permute-start.7 = (f32[128,128]{1,0:T(8,128)S(1)}, f32[128,128]{1,0:T(8,128)S(1)}, u32[]{:S(2)}, u32[]{:S(2)}) collective-permute-start(f32[128,128]{1,0:T(8,128)S(1)} %shard_map.65.refs_0_), channel_id=1, source_target_pairs={{0,16},{8,24},{16,0},{24,8},{1,17},{9,25},{17,1},{25,9},{2,18},{10... | collective-permute-start | bytes 196616 | tf_op jit(solution)/shard_map/ppermute | solution.py:227
  61.5 4.3 %collective-permute-start.8 = (f32[128,128]{1,0:T(8,128)S(1)}, f32[128,128]{1,0:T(8,128)S(1)}, u32[]{:S(2)}, u32[]{:S(2)}) collective-permute-start(f32[128,128]{1,0:T(8,128)S(1)} %shard_map.65.refs_0_), channel_id=1, source_target_pairs={{0,24},{8,16},{16,8},{24,0},{1,25},{9,17},{17,9},{25,1},{2,26},{10... | collective-permute-start | bytes 196616 | tf_op jit(solution)/shard_map/ppermute | solution.py:227
  62.0 8.1 %collective-permute-start.16 = (f32[128,128]{1,0:T(8,128)S(1)}, f32[128,128]{1,0:T(8,128)S(1)}, u32[]{:S(2)}, u32[]{:S(2)}) collective-permute-start(f32[128,128]{1,0:T(8,128)S(1)} %shard_map.68.refs_0_), channel_id=1, source_target_pairs={{0,8},{8,0},{16,24},{24,16},{1,9},{9,1},{17,25},{25,17},{2,10},{10... | collective-permute-start | bytes 196616 | tf_op jit(solution)/shard_map/ppermute | solution.py:227
  63.7 6.4 %collective-permute-start.17 = (f32[128,128]{1,0:T(8,128)S(1)}, f32[128,128]{1,0:T(8,128)S(1)}, u32[]{:S(2)}, u32[]{:S(2)}) collective-permute-start(f32[128,128]{1,0:T(8,128)S(1)} %shard_map.68.refs_0_), channel_id=1, source_target_pairs={{0,16},{8,24},{16,0},{24,8},{1,17},{9,25},{17,1},{25,9},{2,18},{10... | collective-permute-start | bytes 196616 | tf_op jit(solution)/shard_map/ppermute | solution.py:227
  64.2 5.9 %collective-permute-start.18 = (f32[128,128]{1,0:T(8,128)S(1)}, f32[128,128]{1,0:T(8,128)S(1)}, u32[]{:S(2)}, u32[]{:S(2)}) collective-permute-start(f32[128,128]{1,0:T(8,128)S(1)} %shard_map.68.refs_0_), channel_id=1, source_target_pairs={{0,24},{8,16},{16,8},{24,0},{1,25},{9,17},{17,9},{25,1},{2,26},{10... | collective-permute-start | bytes 196616 | tf_op jit(solution)/shard_map/ppermute | solution.py:227
  66.1 7.9 %collective-permute-start.9 = (bf16[64,512]{1,0:T(8,128)(2,1)S(1)}, bf16[64,512]{1,0:T(8,128)(2,1)S(1)}, u32[]{:S(2)}, u32[]{:S(2)}) collective-permute-start(bf16[64,512]{1,0:T(8,128)(2,1)S(1)} %get-tuple-element.54), channel_id=1, source_target_pairs={{0,1},{1,0},{2,3},{3,2},{4,5},{5,4},{6,7},{7,6},{8,9},{9,8},{10,11... | collective-permute-start | bytes 196616 | tf_op jit(solution)/shard_map/ppermute | solution.py:227
  66.1 7.8 %collective-permute-start.10 = (bf16[64,512]{1,0:T(8,128)(2,1)S(1)}, bf16[64,512]{1,0:T(8,128)(2,1)S(1)}, u32[]{:S(2)}, u32[]{:S(2)}) collective-permute-start(bf16[64,512]{1,0:T(8,128)(2,1)S(1)} %get-tuple-element.55), channel_id=1, source_target_pairs={{0,2},{1,3},{2,0},{3,1},{4,6},{5,7},{6,4},{7,5},{8,10},{9,11},{10,... | collective-permute-start | bytes 196616 | tf_op jit(solution)/shard_map/ppermute | solution.py:227
  70.1 5.3 %collective-permute-start.11 = (bf16[64,512]{1,0:T(8,128)(2,1)S(1)}, bf16[64,512]{1,0:T(8,128)(2,1)S(1)}, u32[]{:S(2)}, u32[]{:S(2)}) collective-permute-start(bf16[64,512]{1,0:T(8,128)(2,1)S(1)} %get-tuple-element.56), channel_id=1, source_target_pairs={{0,3},{1,2},{2,1},{3,0},{4,7},{5,6},{6,5},{7,4},{8,11},{9,10},{10,... | collective-permute-start | bytes 196616 | tf_op jit(solution)/shard_map/ppermute | solution.py:227
  70.4 5.2 %collective-permute-start.20 = (bf16[64,512]{1,0:T(8,128)(2,1)S(1)}, bf16[64,512]{1,0:T(8,128)(2,1)S(1)}, u32[]{:S(2)}, u32[]{:S(2)}) collective-permute-start(bf16[64,512]{1,0:T(8,128)(2,1)S(1)} %get-tuple-element.64), channel_id=1, source_target_pairs={{0,1},{1,0},{2,3},{3,2},{4,5},{5,4},{6,7},{7,6},{8,9},{9,8},{10,11... | collective-permute-start | bytes 196616 | tf_op jit(solution)/shard_map/ppermute | solution.py:227
  72.0 4.7 %collective-permute-start.21 = (bf16[64,512]{1,0:T(8,128)(2,1)S(1)}, bf16[64,512]{1,0:T(8,128)(2,1)S(1)}, u32[]{:S(2)}, u32[]{:S(2)}) collective-permute-start(bf16[64,512]{1,0:T(8,128)(2,1)S(1)} %get-tuple-element.65), channel_id=1, source_target_pairs={{0,2},{1,3},{2,0},{3,1},{4,6},{5,7},{6,4},{7,5},{8,10},{9,11},{10,... | collective-permute-start | bytes 196616 | tf_op jit(solution)/shard_map/ppermute | solution.py:227
  73.9 5.2 %collective-permute-start.22 = (bf16[64,512]{1,0:T(8,128)(2,1)S(1)}, bf16[64,512]{1,0:T(8,128)(2,1)S(1)}, u32[]{:S(2)}, u32[]{:S(2)}) collective-permute-start(bf16[64,512]{1,0:T(8,128)(2,1)S(1)} %get-tuple-element.66), channel_id=1, source_target_pairs={{0,3},{1,2},{2,1},{3,0},{4,7},{5,6},{6,5},{7,4},{8,11},{9,10},{10,... | collective-permute-start | bytes 196616 | tf_op jit(solution)/shard_map/ppermute | solution.py:227

commit v2 on v1

--- a/solution.py
+++ b/solution.py
@@ -147,8 +147,8 @@
     )(*blocks, code, down)[0]
 
 
-def raise_kernel(pool, count, *refs):
-    partial_refs, (code_ref, up_ref), out_refs = refs[:count], refs[count : count + 2], refs[count + 2 :]
+def place_kernel(pool, count, *refs):
+    partial_refs, (code_ref, placed_ref) = refs[:count], refs[count:]
     ranks = partial_refs[0][...]
     for ref in partial_refs[1:]:
         ranks = ranks + ref[...]
@@ -164,8 +164,11 @@
         jnp.where(member == jnp.where(upper, 2.0 * pair + 1.0, 2.0 * pair), ranks, 0.0)
         for pair in range(pool // 2)
     ]
-    placed = jnp.concatenate(placed, axis=1).astype(jnp.bfloat16)
-    raised = jnp.dot(placed, up_ref[...], preferred_element_type=jnp.float32)
+    placed_ref[...] = jnp.concatenate(placed, axis=1).astype(jnp.bfloat16)
+
+
+def raise_kernel(placed_ref, up_ref, *out_refs):
+    raised = jnp.dot(placed_ref[...], up_ref[...], preferred_element_type=jnp.float32)
     raised = raised.astype(jnp.bfloat16)
     cap = out_refs[0].shape[0]
     for k, ref in enumerate(out_refs):
@@ -174,10 +177,11 @@
 
 def raise_ranks(partials, code, up, cap, pool):
     outs = code.shape[0] // cap
-    return resident_call(
-        functools.partial(raise_kernel, pool, len(partials)),
-        [((cap, up.shape[1]), jnp.bfloat16)] * outs,
-    )(*partials, code, up)
+    placed = resident_call(
+        functools.partial(place_kernel, pool, len(partials)),
+        [((code.shape[0], up.shape[0]), jnp.bfloat16)],
+    )(*partials, code)[0]
+    return resident_call(raise_kernel, [((cap, up.shape[1]), jnp.bfloat16)] * outs)(placed, up)
 
 
 def join_kernel(spread_ref, base_ref, *refs):

time: 80.2 us -> 80.3 us (level)
  waiting for transfers between devices: 41.3 us -> 39.4 us
  starting transfers between devices: 27.2 us -> 29 us
    ppermute x23, waiting for transfers between devices: 41.3 us -> 39.4 us  [swap(): return lax.ppermute(value, axis, [(i, i ^ apart) for i in range(size)])]
    ppermute x23, starting transfers between devices: 27.2 us -> 29 us  [swap(): return lax.ppermute(value, axis, [(i, i ^ apart) for i in range(size)])]
    pallas_call x6 -> x8, Pallas kernels: 1.9 us -> 2.03 us  [call(): pl.pallas_call(kernel, in_specs=[IN_VMEM] * len(operands), out_specs=[IN_...]
  transfers between devices with their start and end apart: 23 -> 23, of which waited for: 8 -> 7; matrix products, arithmetic and copies ran while one was open for 0% -> 0% of each run, Pallas kernels for 13% -> 13%
where the time goes in v2:
time: 80.3 us; the launch traced here: 80.1 us
  waiting for transfers between devices  39.4 us (49%)
  starting transfers between devices  29 us (36%)
  Pallas kernels  11.5 us (14%)
    ppermute x23, waiting for transfers between devices, swap(): return lax.ppermute(value, axis, [(i, i ^ apart) for i in range(size)])  39.4 us
    ppermute x23, starting transfers between devices, swap(): return lax.ppermute(value, axis, [(i, i ^ apart) for i in range(size)])  29 us
    pallas_call x1, Pallas kernels, base_product(): pl.pallas_call(base_kernel, grid=(steps,), in_specs=[pl.BlockSpec((rows,...  6.46 us
    pallas_call x1, Pallas kernels, pack(): pl.pallas_call(functools.partial(pack_kernel, n, far, cap), in_specs=[IN_...  2.1 us
    pallas_call x8, Pallas kernels, call(): pl.pallas_call(kernel, in_specs=[IN_VMEM] * len(operands), out_specs=[IN_...  2.03 us
  transfers between devices with their start and end apart: 23, of which 7 were waited for; matrix products, arithmetic and copies ran while one was open for 0% of the time, Pallas kernels for 13%

profile of v2, /device:TPU:16, one launch (start us, length us, event | category | flops | bytes accessed | tf_op | source)
XLA Modules:
  0.0 80.1 jit_solution(2741921619816952640)
XLA Ops:
  0.0 0.4 collective-permute-start.15
  0.5 2.1 %pack.1 = (bf16[256,256]{1,0:T(8,128)(2,1)S(1)}, bf16[256,256]{1,0:T(8,128)(2,1)S(1)}, bf16[64,2048]{1,0:T(8,128)(2,1)S(1)}, bf16[64,2048]{1,0:T(8,128)(2,1)S(1)...) custom-call(s32[1,256]{1,0:T(1,128)} %bitcast.2, ...), custom_call_target="tpu_custom_call" | custom-call | tf_op jit(solution)/shard_map/pack/pallas_call | solution.py:93
  2.6 0.0 copy-start.1
  2.6 1.6 %collective-permute-start = (bf16[64,2048]{1,0:T(8,128)(2,1)S(1)}, bf16[64,2048]{1,0:T(8,128)(2,1)S(1)}, u32[]{:S(2)}, u32[]{:S(2)}) collective-permute-start(bf16[64,2048]{1,0:T(8,128)(2,1)S(1)} %get-tuple-element.39), channel_id=1, source_target_pairs={{0,1},{1,0},{2,3},{3,2},{4,5},{5,4},{6,7},{7,6},{8,9},{9,8},{10,11... | collective-permute-start | bytes 786440 | tf_op jit(solution)/shard_map/ppermute | solution.py:231
  4.1 1.3 %collective-permute-start.1 = (bf16[64,2048]{1,0:T(8,128)(2,1)S(1)}, bf16[64,2048]{1,0:T(8,128)(2,1)S(1)}, u32[]{:S(2)}, u32[]{:S(2)}) collective-permute-start(bf16[64,2048]{1,0:T(8,128)(2,1)S(1)} %get-tuple-element.40), channel_id=1, source_target_pairs={{0,2},{1,3},{2,0},{3,1},{4,6},{5,7},{6,4},{7,5},{8,10},{9,11},{10,... | collective-permute-start | bytes 786440 | tf_op jit(solution)/shard_map/ppermute | solution.py:231
  5.5 0.6 collective-permute-start.2
  6.1 1.5 %collective-permute-start.3 = (f32[8,128]{1,0:T(8,128)S(1)}, f32[8,128]{1,0:T(8,128)S(1)}, u32[]{:S(2)}, u32[]{:S(2)}) collective-permute-start(f32[8,128]{1,0:T(8,128)S(1)} %get-tuple-element.48), channel_id=1, source_target_pairs={{0,1},{1,0},{2,3},{3,2},{4,5},{5,4},{6,7},{7,6},{8,9},{9,8},{10,11... | collective-permute-start | bytes 12296 | tf_op jit(solution)/shard_map/ppermute | solution.py:231
  7.6 2.9 %collective-permute-done.3.refs_1_ = f32[8,128]{1,0:T(8,128)S(1)} collective-permute-done((f32[8,128]{1,0:T(8,128)S(1)}, f32[8,128]{1,0:T(8,128)S(1)}, u32[]{:S(2)}, u32[]{:S(2)}) %collective-permute-start.3) | collective-permute-done | bytes 4128 | tf_op jit(solution)/shard_map/ppermute | solution.py:231
  10.5 1.4 %collective-permute-start.4 = (f32[8,128]{1,0:T(8,128)S(1)}, f32[8,128]{1,0:T(8,128)S(1)}, u32[]{:S(2)}, u32[]{:S(2)}) collective-permute-start(f32[8,128]{1,0:T(8,128)S(1)} %get-tuple-element.49), channel_id=1, source_target_pairs={{0,2},{1,3},{2,0},{3,1},{4,6},{5,7},{6,4},{7,5},{8,10},{9,11},{10,... | collective-permute-start | bytes 12296 | tf_op jit(solution)/shard_map/ppermute | solution.py:231
  11.9 25.6 %collective-permute-done.4.refs_2_ = f32[8,128]{1,0:T(8,128)S(1)} collective-permute-done((f32[8,128]{1,0:T(8,128)S(1)}, f32[8,128]{1,0:T(8,128)S(1)}, u32[]{:S(2)}, u32[]{:S(2)}) %collective-permute-start.4) | collective-permute-done | bytes 4128 | tf_op jit(solution)/shard_map/ppermute | solution.py:231
  37.5 3.4 %collective-permute-start.5 = (f32[8,128]{1,0:T(8,128)S(1)}, f32[8,128]{1,0:T(8,128)S(1)}, u32[]{:S(2)}, u32[]{:S(2)}) collective-permute-start(f32[8,128]{1,0:T(8,128)S(1)} %get-tuple-element.50), channel_id=1, source_target_pairs={{0,3},{1,2},{2,1},{3,0},{4,7},{5,6},{6,5},{7,4},{8,11},{9,10},{10,... | collective-permute-start | bytes 12296 | tf_op jit(solution)/shard_map/ppermute | solution.py:231
  40.8 1.6 %collective-permute-done.5.refs_3_ = f32[8,128]{1,0:T(8,128)S(1)} collective-permute-done((f32[8,128]{1,0:T(8,128)S(1)}, f32[8,128]{1,0:T(8,128)S(1)}, u32[]{:S(2)}, u32[]{:S(2)}) %collective-permute-start.5) | collective-permute-done | bytes 4128 | tf_op jit(solution)/shard_map/ppermute | solution.py:231
  42.4 1.0 %collective-permute-start.12 = (bf16[64,2048]{1,0:T(8,128)(2,1)S(1)}, bf16[64,2048]{1,0:T(8,128)(2,1)S(1)}, u32[]{:S(2)}, u32[]{:S(2)}) collective-permute-start(bf16[64,2048]{1,0:T(8,128)(2,1)S(1)} %get-tuple-element.58), channel_id=1, source_target_pairs={{0,1},{1,0},{2,3},{3,2},{4,5},{5,4},{6,7},{7,6},{8,9},{9,8},{10,11... | collective-permute-start | bytes 786440 | tf_op jit(solution)/shard_map/ppermute | solution.py:231
  43.5 0.0 collective-permute-done.refs_1_
  43.5 2.5 %collective-permute-start.13 = (bf16[64,2048]{1,0:T(8,128)(2,1)S(1)}, bf16[64,2048]{1,0:T(8,128)(2,1)S(1)}, u32[]{:S(2)}, u32[]{:S(2)}) collective-permute-start(bf16[64,2048]{1,0:T(8,128)(2,1)S(1)} %get-tuple-element.59), channel_id=1, source_target_pairs={{0,2},{1,3},{2,0},{3,1},{4,6},{5,7},{6,4},{7,5},{8,10},{9,11},{10,... | collective-permute-start | bytes 786440 | tf_op jit(solution)/shard_map/ppermute | solution.py:231
  45.9 0.0 collective-permute-start.14
  46.0 6.5 %base_product.1.base_ref = f32[256,512]{1,0:T(8,128)S(1)} custom-call(bf16[256,8192]{1,0:T(8,128)(2,1)} %hidden_ref.3, bf16[8192,512]{1,0:T(8,128)(2,1)} %weight_ref.1), custom_call_target="tpu_custom_call" | custom-call | tf_op jit(solution)/shard_map/base_product/pallas_call | solution.py:216
  52.4 0.1 shard_map.64
  52.6 0.5 shard_map.65.refs_0_
  53.1 1.1 %collective-permute-start.19 = (bf16[256,512]{1,0:T(8,128)(2,1)S(1)}, bf16[256,512]{1,0:T(8,128)(2,1)S(1)}, u32[]{:S(2)}, u32[]{:S(2)}) collective-permute-start(bf16[256,512]{1,0:T(8,128)(2,1)S(1)} %copy-done.1), channel_id=1, source_target_pairs={{0,6},{1,7},{2,4},{3,5},{4,2},{5,3},{6,0},{7,1},{8,14},{9,15},{10,... | collective-permute-start | bytes 786440 | tf_op jit(solution)/shard_map/ppermute | solution.py:231
  54.2 0.0 collective-permute-done.12.refs_1_
  54.2 1.6 %collective-permute-start.7 = (f32[128,128]{1,0:T(8,128)S(1)}, f32[128,128]{1,0:T(8,128)S(1)}, u32[]{:S(2)}, u32[]{:S(2)}) collective-permute-start(f32[128,128]{1,0:T(8,128)S(1)} %shard_map.65.refs_0_), channel_id=1, source_target_pairs={{0,16},{8,24},{16,0},{24,8},{1,17},{9,25},{17,1},{25,9},{2,18},{10... | collective-permute-start | bytes 196616 | tf_op jit(solution)/shard_map/ppermute | solution.py:231
  55.8 5.6 %collective-permute-done.14.refs_3_ = bf16[64,2048]{1,0:T(8,128)(2,1)S(1)} collective-permute-done((bf16[64,2048]{1,0:T(8,128)(2,1)S(1)}, bf16[64,2048]{1,0:T(8,128)(2,1)S(1)}, u32[]{:S(2)}, u32[]{:S(2)}) %collective-permute-start.14) | collective-permute-done | bytes 262176 | tf_op jit(solution)/shard_map/ppermute | solution.py:231
  61.5 0.0 collective-permute-start.8
  61.5 0.0 collective-permute-done.15.refs_5_
  61.5 0.5 shard_map.69.refs_0_
  62.0 1.7 %collective-permute-start.16 = (f32[128,128]{1,0:T(8,128)S(1)}, f32[128,128]{1,0:T(8,128)S(1)}, u32[]{:S(2)}, u32[]{:S(2)}) collective-permute-start(f32[128,128]{1,0:T(8,128)S(1)} %shard_map.69.refs_0_), channel_id=1, source_target_pairs={{0,8},{8,0},{16,24},{24,16},{1,9},{9,1},{17,25},{25,17},{2,10},{10... | collective-permute-start | bytes 196616 | tf_op jit(solution)/shard_map/ppermute | solution.py:231
  63.7 0.0 collective-permute-done.6.refs_1_
  63.7 0.5 collective-permute-start.17
  64.2 0.0 collective-permute-done.7.refs_2_
  64.2 0.9 %collective-permute-start.18 = (f32[128,128]{1,0:T(8,128)S(1)}, f32[128,128]{1,0:T(8,128)S(1)}, u32[]{:S(2)}, u32[]{:S(2)}) collective-permute-start(f32[128,128]{1,0:T(8,128)S(1)} %shard_map.69.refs_0_), channel_id=1, source_target_pairs={{0,24},{8,16},{16,8},{24,0},{1,25},{9,17},{17,9},{25,1},{2,26},{10... | collective-permute-start | bytes 196616 | tf_op jit(solution)/shard_map/ppermute | solution.py:231
  65.1 0.7 collective-permute-done.8.refs_3_
  65.8 0.1 shard_map.66.placed_ref
  65.9 0.2 shard_map.67
  66.1 0.1 collective-permute-start.9
  66.2 0.0 collective-permute-done.16.refs_1_
  66.2 3.9 %collective-permute-start.10 = (bf16[64,512]{1,0:T(8,128)(2,1)S(1)}, bf16[64,512]{1,0:T(8,128)(2,1)S(1)}, u32[]{:S(2)}, u32[]{:S(2)}) collective-permute-start(bf16[64,512]{1,0:T(8,128)(2,1)S(1)} %get-tuple-element.55), channel_id=1, source_target_pairs={{0,2},{1,3},{2,0},{3,1},{4,6},{5,7},{6,4},{7,5},{8,10},{9,11},{10,... | collective-permute-start | bytes 196616 | tf_op jit(solution)/shard_map/ppermute | solution.py:231
  70.1 1.8 %collective-permute-start.11 = (bf16[64,512]{1,0:T(8,128)(2,1)S(1)}, bf16[64,512]{1,0:T(8,128)(2,1)S(1)}, u32[]{:S(2)}, u32[]{:S(2)}) collective-permute-start(bf16[64,512]{1,0:T(8,128)(2,1)S(1)} %get-tuple-element.56), channel_id=1, source_target_pairs={{0,3},{1,2},{2,1},{3,0},{4,7},{5,6},{6,5},{7,4},{8,11},{9,10},{10,... | collective-permute-start | bytes 196616 | tf_op jit(solution)/shard_map/ppermute | solution.py:231
  72.0 0.0 collective-permute-done.18.refs_3_
  72.0 0.1 shard_map.70.placed_ref
  72.1 0.2 shard_map.71
  72.3 0.1 collective-permute-start.20
  72.4 1.6 %collective-permute-start.21 = (bf16[64,512]{1,0:T(8,128)(2,1)S(1)}, bf16[64,512]{1,0:T(8,128)(2,1)S(1)}, u32[]{:S(2)}, u32[]{:S(2)}) collective-permute-start(bf16[64,512]{1,0:T(8,128)(2,1)S(1)} %get-tuple-element.65), channel_id=1, source_target_pairs={{0,2},{1,3},{2,0},{3,1},{4,6},{5,7},{6,4},{7,5},{8,10},{9,11},{10,... | collective-permute-start | bytes 196616 | tf_op jit(solution)/shard_map/ppermute | solution.py:231
  74.0 1.8 %collective-permute-start.22 = (bf16[64,512]{1,0:T(8,128)(2,1)S(1)}, bf16[64,512]{1,0:T(8,128)(2,1)S(1)}, u32[]{:S(2)}, u32[]{:S(2)}) collective-permute-start(bf16[64,512]{1,0:T(8,128)(2,1)S(1)} %get-tuple-element.66), channel_id=1, source_target_pairs={{0,3},{1,2},{2,1},{3,0},{4,7},{5,6},{6,5},{7,4},{8,11},{9,10},{10,... | collective-permute-start | bytes 196616 | tf_op jit(solution)/shard_map/ppermute | solution.py:231
  75.9 0.2 shard_map.68.base_ref
  76.1 1.2 %collective-permute-done.20.refs_1_ = bf16[64,512]{1,0:T(8,128)(2,1)S(1)} collective-permute-done((bf16[64,512]{1,0:T(8,128)(2,1)S(1)}, bf16[64,512]{1,0:T(8,128)(2,1)S(1)}, u32[]{:S(2)}, u32[]{:S(2)}) %collective-permute-start.20) | collective-permute-done | bytes 65568 | tf_op jit(solution)/shard_map/ppermute | solution.py:231
  77.4 1.8 %collective-permute-done.22.refs_3_ = bf16[64,512]{1,0:T(8,128)(2,1)S(1)} collective-permute-done((bf16[64,512]{1,0:T(8,128)(2,1)S(1)}, bf16[64,512]{1,0:T(8,128)(2,1)S(1)}, u32[]{:S(2)}, u32[]{:S(2)}) %collective-permute-start.22) | collective-permute-done | bytes 65568 | tf_op jit(solution)/shard_map/ppermute | solution.py:231
  79.2 0.9 %shard_map.72 = bf16[256,512]{1,0:T(8,128)(2,1)} custom-call(bf16[256,256]{1,0:T(8,128)(2,1)S(1)} %get-tuple-element.36.spread_ref, f32[256,512]{1,0:T(8,128)S(1)} %shard_map.68.base_ref, bf16[64,512]{1,0:T(8,128)(2,1)S(1)} %get-tuple-element.63.refs_0_, bf16[64,512]{1,0:T(8,128)(2,1)S(1)} %collective-permute-done.20.refs_1_, ...), custom_call_target="tpu_custom_call" | custom-call | tf_op jit(solution)/shard_map/pallas_call | solution.py:197
  (13 shorter events, 0.0 us)
Async XLA Ops:
  0.0 61.5 %collective-permute-start.15 = (bf16[2048,256]{1,0:T(8,128)(2,1)}, bf16[2048,256]{1,0:T(8,128)(2,1)S(1)}, u32[]{:S(2)}, u32[]{:S(2)}) collective-permute-start(bf16[2048,256]{1,0:T(8,128)(2,1)} %refs_5_.1), channel_id=1, source_target_pairs={{0,6},{1,7},{2,4},{3,5},{4,2},{5,3},{6,0},{7,1},{8,14},{9,15},{10,... | collective-permute-start | bytes 3145736 | tf_op jit(solution)/shard_map/ppermute | solution.py:231
  0.5 52.1 %copy-start = (bf16[2048,256]{1,0:T(8,128)(2,1)S(1)}, bf16[2048,256]{1,0:T(8,128)(2,1)}, u32[]{:S(2)}) copy-start(bf16[2048,256]{1,0:T(8,128)(2,1)} %refs_5_.1) | copy-start | bytes 3145732
  2.6 50.5 %copy-start.1 = (bf16[256,512]{1,0:T(8,128)(2,1)S(1)}, bf16[256,512]{1,0:T(8,128)(2,1)}, u32[]{:S(2)}) copy-start(bf16[256,512]{1,0:T(8,128)(2,1)} %up_ref.1) | copy-start | bytes 786436
  2.6 40.9 %collective-permute-start = (bf16[64,2048]{1,0:T(8,128)(2,1)S(1)}, bf16[64,2048]{1,0:T(8,128)(2,1)S(1)}, u32[]{:S(2)}, u32[]{:S(2)}) collective-permute-start(bf16[64,2048]{1,0:T(8,128)(2,1)S(1)} %get-tuple-element.39), channel_id=1, source_target_pairs={{0,1},{1,0},{2,3},{3,2},{4,5},{5,4},{6,7},{7,6},{8,9},{9,8},{10,11... | collective-permute-start | bytes 786440 | tf_op jit(solution)/shard_map/ppermute | solution.py:231
  4.1 41.8 %collective-permute-start.1 = (bf16[64,2048]{1,0:T(8,128)(2,1)S(1)}, bf16[64,2048]{1,0:T(8,128)(2,1)S(1)}, u32[]{:S(2)}, u32[]{:S(2)}) collective-permute-start(bf16[64,2048]{1,0:T(8,128)(2,1)S(1)} %get-tuple-element.40), channel_id=1, source_target_pairs={{0,2},{1,3},{2,0},{3,1},{4,6},{5,7},{6,4},{7,5},{8,10},{9,11},{10,... | collective-permute-start | bytes 786440 | tf_op jit(solution)/shard_map/ppermute | solution.py:231
  5.5 47.1 %collective-permute-start.2 = (bf16[64,2048]{1,0:T(8,128)(2,1)S(1)}, bf16[64,2048]{1,0:T(8,128)(2,1)S(1)}, u32[]{:S(2)}, u32[]{:S(2)}) collective-permute-start(bf16[64,2048]{1,0:T(8,128)(2,1)S(1)} %get-tuple-element.41), channel_id=1, source_target_pairs={{0,3},{1,2},{2,1},{3,0},{4,7},{5,6},{6,5},{7,4},{8,11},{9,10},{10,... | collective-permute-start | bytes 786440 | tf_op jit(solution)/shard_map/ppermute | solution.py:231
  6.1 4.4 %collective-permute-start.3 = (f32[8,128]{1,0:T(8,128)S(1)}, f32[8,128]{1,0:T(8,128)S(1)}, u32[]{:S(2)}, u32[]{:S(2)}) collective-permute-start(f32[8,128]{1,0:T(8,128)S(1)} %get-tuple-element.48), channel_id=1, source_target_pairs={{0,1},{1,0},{2,3},{3,2},{4,5},{5,4},{6,7},{7,6},{8,9},{9,8},{10,11... | collective-permute-start | bytes 12296 | tf_op jit(solution)/shard_map/ppermute | solution.py:231
  10.5 27.0 %collective-permute-start.4 = (f32[8,128]{1,0:T(8,128)S(1)}, f32[8,128]{1,0:T(8,128)S(1)}, u32[]{:S(2)}, u32[]{:S(2)}) collective-permute-start(f32[8,128]{1,0:T(8,128)S(1)} %get-tuple-element.49), channel_id=1, source_target_pairs={{0,2},{1,3},{2,0},{3,1},{4,6},{5,7},{6,4},{7,5},{8,10},{9,11},{10,... | collective-permute-start | bytes 12296 | tf_op jit(solution)/shard_map/ppermute | solution.py:231
  37.5 5.0 %collective-permute-start.5 = (f32[8,128]{1,0:T(8,128)S(1)}, f32[8,128]{1,0:T(8,128)S(1)}, u32[]{:S(2)}, u32[]{:S(2)}) collective-permute-start(f32[8,128]{1,0:T(8,128)S(1)} %get-tuple-element.50), channel_id=1, source_target_pairs={{0,3},{1,2},{2,1},{3,0},{4,7},{5,6},{6,5},{7,4},{8,11},{9,10},{10,... | collective-permute-start | bytes 12296 | tf_op jit(solution)/shard_map/ppermute | solution.py:231
  42.4 11.8 %collective-permute-start.12 = (bf16[64,2048]{1,0:T(8,128)(2,1)S(1)}, bf16[64,2048]{1,0:T(8,128)(2,1)S(1)}, u32[]{:S(2)}, u32[]{:S(2)}) collective-permute-start(bf16[64,2048]{1,0:T(8,128)(2,1)S(1)} %get-tuple-element.58), channel_id=1, source_target_pairs={{0,1},{1,0},{2,3},{3,2},{4,5},{5,4},{6,7},{7,6},{8,9},{9,8},{10,11... | collective-permute-start | bytes 786440 | tf_op jit(solution)/shard_map/ppermute | solution.py:231
  43.5 10.8 %collective-permute-start.13 = (bf16[64,2048]{1,0:T(8,128)(2,1)S(1)}, bf16[64,2048]{1,0:T(8,128)(2,1)S(1)}, u32[]{:S(2)}, u32[]{:S(2)}) collective-permute-start(bf16[64,2048]{1,0:T(8,128)(2,1)S(1)} %get-tuple-element.59), channel_id=1, source_target_pairs={{0,2},{1,3},{2,0},{3,1},{4,6},{5,7},{6,4},{7,5},{8,10},{9,11},{10,... | collective-permute-start | bytes 786440 | tf_op jit(solution)/shard_map/ppermute | solution.py:231
  45.9 15.5 %collective-permute-start.14 = (bf16[64,2048]{1,0:T(8,128)(2,1)S(1)}, bf16[64,2048]{1,0:T(8,128)(2,1)S(1)}, u32[]{:S(2)}, u32[]{:S(2)}) collective-permute-start(bf16[64,2048]{1,0:T(8,128)(2,1)S(1)} %get-tuple-element.60), channel_id=1, source_target_pairs={{0,3},{1,2},{2,1},{3,0},{4,7},{5,6},{6,5},{7,4},{8,11},{9,10},{10,... | collective-permute-start | bytes 786440 | tf_op jit(solution)/shard_map/ppermute | solution.py:231
  53.1 19.0 %collective-permute-start.19 = (bf16[256,512]{1,0:T(8,128)(2,1)S(1)}, bf16[256,512]{1,0:T(8,128)(2,1)S(1)}, u32[]{:S(2)}, u32[]{:S(2)}) collective-permute-start(bf16[256,512]{1,0:T(8,128)(2,1)S(1)} %copy-done.1), channel_id=1, source_target_pairs={{0,6},{1,7},{2,4},{3,5},{4,2},{5,3},{6,0},{7,1},{8,14},{9,15},{10,... | collective-permute-start | bytes 786440 | tf_op jit(solution)/shard_map/ppermute | solution.py:231
  54.2 9.5 %collective-permute-start.6 = (f32[128,128]{1,0:T(8,128)S(1)}, f32[128,128]{1,0:T(8,128)S(1)}, u32[]{:S(2)}, u32[]{:S(2)}) collective-permute-start(f32[128,128]{1,0:T(8,128)S(1)} %shard_map.65.refs_0_), channel_id=1, source_target_pairs={{0,8},{8,0},{16,24},{24,16},{1,9},{9,1},{17,25},{25,17},{2,10},{10... | collective-permute-start | bytes 196616 | tf_op jit(solution)/shard_map/ppermute | solution.py:231
  54.2 10.0 %collective-permute-start.7 = (f32[128,128]{1,0:T(8,128)S(1)}, f32[128,128]{1,0:T(8,128)S(1)}, u32[]{:S(2)}, u32[]{:S(2)}) collective-permute-start(f32[128,128]{1,0:T(8,128)S(1)} %shard_map.65.refs_0_), channel_id=1, source_target_pairs={{0,16},{8,24},{16,0},{24,8},{1,17},{9,25},{17,1},{25,9},{2,18},{10... | collective-permute-start | bytes 196616 | tf_op jit(solution)/shard_map/ppermute | solution.py:231
  61.5 4.3 %collective-permute-start.8 = (f32[128,128]{1,0:T(8,128)S(1)}, f32[128,128]{1,0:T(8,128)S(1)}, u32[]{:S(2)}, u32[]{:S(2)}) collective-permute-start(f32[128,128]{1,0:T(8,128)S(1)} %shard_map.65.refs_0_), channel_id=1, source_target_pairs={{0,24},{8,16},{16,8},{24,0},{1,25},{9,17},{17,9},{25,1},{2,26},{10... | collective-permute-start | bytes 196616 | tf_op jit(solution)/shard_map/ppermute | solution.py:231
  62.0 4.2 %collective-permute-start.16 = (f32[128,128]{1,0:T(8,128)S(1)}, f32[128,128]{1,0:T(8,128)S(1)}, u32[]{:S(2)}, u32[]{:S(2)}) collective-permute-start(f32[128,128]{1,0:T(8,128)S(1)} %shard_map.69.refs_0_), channel_id=1, source_target_pairs={{0,8},{8,0},{16,24},{24,16},{1,9},{9,1},{17,25},{25,17},{2,10},{10... | collective-permute-start | bytes 196616 | tf_op jit(solution)/shard_map/ppermute | solution.py:231
  63.7 6.4 %collective-permute-start.17 = (f32[128,128]{1,0:T(8,128)S(1)}, f32[128,128]{1,0:T(8,128)S(1)}, u32[]{:S(2)}, u32[]{:S(2)}) collective-permute-start(f32[128,128]{1,0:T(8,128)S(1)} %shard_map.69.refs_0_), channel_id=1, source_target_pairs={{0,16},{8,24},{16,0},{24,8},{1,17},{9,25},{17,1},{25,9},{2,18},{10... | collective-permute-start | bytes 196616 | tf_op jit(solution)/shard_map/ppermute | solution.py:231
  64.2 7.8 %collective-permute-start.18 = (f32[128,128]{1,0:T(8,128)S(1)}, f32[128,128]{1,0:T(8,128)S(1)}, u32[]{:S(2)}, u32[]{:S(2)}) collective-permute-start(f32[128,128]{1,0:T(8,128)S(1)} %shard_map.69.refs_0_), channel_id=1, source_target_pairs={{0,24},{8,16},{16,8},{24,0},{1,25},{9,17},{17,9},{25,1},{2,26},{10... | collective-permute-start | bytes 196616 | tf_op jit(solution)/shard_map/ppermute | solution.py:231
  66.1 7.9 %collective-permute-start.9 = (bf16[64,512]{1,0:T(8,128)(2,1)S(1)}, bf16[64,512]{1,0:T(8,128)(2,1)S(1)}, u32[]{:S(2)}, u32[]{:S(2)}) collective-permute-start(bf16[64,512]{1,0:T(8,128)(2,1)S(1)} %get-tuple-element.54), channel_id=1, source_target_pairs={{0,1},{1,0},{2,3},{3,2},{4,5},{5,4},{6,7},{7,6},{8,9},{9,8},{10,11... | collective-permute-start | bytes 196616 | tf_op jit(solution)/shard_map/ppermute | solution.py:231
  66.2 9.7 %collective-permute-start.10 = (bf16[64,512]{1,0:T(8,128)(2,1)S(1)}, bf16[64,512]{1,0:T(8,128)(2,1)S(1)}, u32[]{:S(2)}, u32[]{:S(2)}) collective-permute-start(bf16[64,512]{1,0:T(8,128)(2,1)S(1)} %get-tuple-element.55), channel_id=1, source_target_pairs={{0,2},{1,3},{2,0},{3,1},{4,6},{5,7},{6,4},{7,5},{8,10},{9,11},{10,... | collective-permute-start | bytes 196616 | tf_op jit(solution)/shard_map/ppermute | solution.py:231
  70.1 5.8 %collective-permute-start.11 = (bf16[64,512]{1,0:T(8,128)(2,1)S(1)}, bf16[64,512]{1,0:T(8,128)(2,1)S(1)}, u32[]{:S(2)}, u32[]{:S(2)}) collective-permute-start(bf16[64,512]{1,0:T(8,128)(2,1)S(1)} %get-tuple-element.56), channel_id=1, source_target_pairs={{0,3},{1,2},{2,1},{3,0},{4,7},{5,6},{6,5},{7,4},{8,11},{9,10},{10,... | collective-permute-start | bytes 196616 | tf_op jit(solution)/shard_map/ppermute | solution.py:231
  72.3 5.0 %collective-permute-start.20 = (bf16[64,512]{1,0:T(8,128)(2,1)S(1)}, bf16[64,512]{1,0:T(8,128)(2,1)S(1)}, u32[]{:S(2)}, u32[]{:S(2)}) collective-permute-start(bf16[64,512]{1,0:T(8,128)(2,1)S(1)} %get-tuple-element.64), channel_id=1, source_target_pairs={{0,1},{1,0},{2,3},{3,2},{4,5},{5,4},{6,7},{7,6},{8,9},{9,8},{10,11... | collective-permute-start | bytes 196616 | tf_op jit(solution)/shard_map/ppermute | solution.py:231
  72.4 5.0 %collective-permute-start.21 = (bf16[64,512]{1,0:T(8,128)(2,1)S(1)}, bf16[64,512]{1,0:T(8,128)(2,1)S(1)}, u32[]{:S(2)}, u32[]{:S(2)}) collective-permute-start(bf16[64,512]{1,0:T(8,128)(2,1)S(1)} %get-tuple-element.65), channel_id=1, source_target_pairs={{0,2},{1,3},{2,0},{3,1},{4,6},{5,7},{6,4},{7,5},{8,10},{9,11},{10,... | collective-permute-start | bytes 196616 | tf_op jit(solution)/shard_map/ppermute | solution.py:231
  74.0 5.2 %collective-permute-start.22 = (bf16[64,512]{1,0:T(8,128)(2,1)S(1)}, bf16[64,512]{1,0:T(8,128)(2,1)S(1)}, u32[]{:S(2)}, u32[]{:S(2)}) collective-permute-start(bf16[64,512]{1,0:T(8,128)(2,1)S(1)} %get-tuple-element.66), channel_id=1, source_target_pairs={{0,3},{1,2},{2,1},{3,0},{4,7},{5,6},{6,5},{7,4},{8,11},{9,10},{10,... | collective-permute-start | bytes 196616 | tf_op jit(solution)/shard_map/ppermute | solution.py:231

commit v3 on v2

--- a/solution.py
+++ b/solution.py
@@ -167,10 +167,11 @@
     placed_ref[...] = jnp.concatenate(placed, axis=1).astype(jnp.bfloat16)
 
 
-def raise_kernel(placed_ref, up_ref, *out_refs):
-    raised = jnp.dot(placed_ref[...], up_ref[...], preferred_element_type=jnp.float32)
+def raise_kernel(first, placed_ref, up_ref, *out_refs):
+    cap = out_refs[0].shape[0]
+    part = placed_ref[first * cap : (first + len(out_refs)) * cap]
+    raised = jnp.dot(part, up_ref[...], preferred_element_type=jnp.float32)
     raised = raised.astype(jnp.bfloat16)
-    cap = out_refs[0].shape[0]
     for k, ref in enumerate(out_refs):
         ref[...] = raised[k * cap : (k + 1) * cap]
 
@@ -181,7 +182,10 @@
         functools.partial(place_kernel, pool, len(partials)),
         [((code.shape[0], up.shape[0]), jnp.bfloat16)],
     )(*partials, code)[0]
-    return resident_call(raise_kernel, [((cap, up.shape[1]), jnp.bfloat16)] * outs)(placed, up)
+    block = [((cap, up.shape[1]), jnp.bfloat16)]
+    last = resident_call(functools.partial(raise_kernel, outs - 1), block)(placed, up)
+    rest = resident_call(functools.partial(raise_kernel, 0), block * (outs - 1))(placed, up)
+    return list(rest) + list(last)
 
 
 def join_kernel(spread_ref, base_ref, *refs):

time: 80.3 us -> 80.7 us (level)
    pallas_call x8 -> x10, Pallas kernels: 2.03 us -> 2.3 us  [call(): pl.pallas_call(kernel, in_specs=[IN_VMEM] * len(operands), out_specs=[IN_...]
  transfers between devices with their start and end apart: 23 -> 23, of which waited for: 7 -> 8; matrix products, arithmetic and copies ran while one was open for 0% -> 0% of each run, Pallas kernels for 13% -> 13%
where the time goes in v3:
time: 80.7 us; the launch traced here: 80.6 us
  waiting for transfers between devices  39.7 us (49%)
  starting transfers between devices  28.9 us (36%)
  Pallas kernels  11.8 us (15%)
    ppermute x23, waiting for transfers between devices, swap(): return lax.ppermute(value, axis, [(i, i ^ apart) for i in range(size)])  39.7 us
    ppermute x23, starting transfers between devices, swap(): return lax.ppermute(value, axis, [(i, i ^ apart) for i in range(size)])  28.9 us
    pallas_call x1, Pallas kernels, base_product(): pl.pallas_call(base_kernel, grid=(steps,), in_specs=[pl.BlockSpec((rows,...  6.46 us
    pallas_call x10, Pallas kernels, call(): pl.pallas_call(kernel, in_specs=[IN_VMEM] * len(operands), out_specs=[IN_...  2.3 us
    pallas_call x1, Pallas kernels, pack(): pl.pallas_call(functools.partial(pack_kernel, n, far, cap), in_specs=[IN_...  2.1 us
  transfers between devices with their start and end apart: 23, of which 8 were waited for; matrix products, arithmetic and copies ran while one was open for 0% of the time, Pallas kernels for 13%

profile of v3, /device:TPU:16, one launch (start us, length us, event | category | flops | bytes accessed | tf_op | source)
XLA Modules:
  0.0 80.6 jit_solution(11232417299048136294)
XLA Ops:
  0.0 0.4 collective-permute-start.15
  0.5 2.1 %pack.1 = (bf16[256,256]{1,0:T(8,128)(2,1)S(1)}, bf16[256,256]{1,0:T(8,128)(2,1)S(1)}, bf16[64,2048]{1,0:T(8,128)(2,1)S(1)}, bf16[64,2048]{1,0:T(8,128)(2,1)S(1)...) custom-call(s32[1,256]{1,0:T(1,128)} %bitcast.2, ...), custom_call_target="tpu_custom_call" | custom-call | tf_op jit(solution)/shard_map/pack/pallas_call | solution.py:93
  2.6 0.0 copy-start
  2.6 1.6 %collective-permute-start = (bf16[64,2048]{1,0:T(8,128)(2,1)S(1)}, bf16[64,2048]{1,0:T(8,128)(2,1)S(1)}, u32[]{:S(2)}, u32[]{:S(2)}) collective-permute-start(bf16[64,2048]{1,0:T(8,128)(2,1)S(1)} %get-tuple-element.37), channel_id=1, source_target_pairs={{0,1},{1,0},{2,3},{3,2},{4,5},{5,4},{6,7},{7,6},{8,9},{9,8},{10,11... | collective-permute-start | bytes 786440 | tf_op jit(solution)/shard_map/ppermute | solution.py:235
  4.1 1.3 %collective-permute-start.1 = (bf16[64,2048]{1,0:T(8,128)(2,1)S(1)}, bf16[64,2048]{1,0:T(8,128)(2,1)S(1)}, u32[]{:S(2)}, u32[]{:S(2)}) collective-permute-start(bf16[64,2048]{1,0:T(8,128)(2,1)S(1)} %get-tuple-element.38), channel_id=1, source_target_pairs={{0,2},{1,3},{2,0},{3,1},{4,6},{5,7},{6,4},{7,5},{8,10},{9,11},{10,... | collective-permute-start | bytes 786440 | tf_op jit(solution)/shard_map/ppermute | solution.py:235
  5.5 0.6 collective-permute-start.2
  6.1 1.5 %collective-permute-start.3 = (f32[8,128]{1,0:T(8,128)S(1)}, f32[8,128]{1,0:T(8,128)S(1)}, u32[]{:S(2)}, u32[]{:S(2)}) collective-permute-start(f32[8,128]{1,0:T(8,128)S(1)} %get-tuple-element.46), channel_id=1, source_target_pairs={{0,1},{1,0},{2,3},{3,2},{4,5},{5,4},{6,7},{7,6},{8,9},{9,8},{10,11... | collective-permute-start | bytes 12296 | tf_op jit(solution)/shard_map/ppermute | solution.py:235
  7.6 2.9 %collective-permute-done.3.refs_1_ = f32[8,128]{1,0:T(8,128)S(1)} collective-permute-done((f32[8,128]{1,0:T(8,128)S(1)}, f32[8,128]{1,0:T(8,128)S(1)}, u32[]{:S(2)}, u32[]{:S(2)}) %collective-permute-start.3) | collective-permute-done | bytes 4128 | tf_op jit(solution)/shard_map/ppermute | solution.py:235
  10.5 1.4 %collective-permute-start.4 = (f32[8,128]{1,0:T(8,128)S(1)}, f32[8,128]{1,0:T(8,128)S(1)}, u32[]{:S(2)}, u32[]{:S(2)}) collective-permute-start(f32[8,128]{1,0:T(8,128)S(1)} %get-tuple-element.47), channel_id=1, source_target_pairs={{0,2},{1,3},{2,0},{3,1},{4,6},{5,7},{6,4},{7,5},{8,10},{9,11},{10,... | collective-permute-start | bytes 12296 | tf_op jit(solution)/shard_map/ppermute | solution.py:235
  11.9 25.6 %collective-permute-done.4.refs_2_ = f32[8,128]{1,0:T(8,128)S(1)} collective-permute-done((f32[8,128]{1,0:T(8,128)S(1)}, f32[8,128]{1,0:T(8,128)S(1)}, u32[]{:S(2)}, u32[]{:S(2)}) %collective-permute-start.4) | collective-permute-done | bytes 4128 | tf_op jit(solution)/shard_map/ppermute | solution.py:235
  37.5 3.4 %collective-permute-start.5 = (f32[8,128]{1,0:T(8,128)S(1)}, f32[8,128]{1,0:T(8,128)S(1)}, u32[]{:S(2)}, u32[]{:S(2)}) collective-permute-start(f32[8,128]{1,0:T(8,128)S(1)} %get-tuple-element.48), channel_id=1, source_target_pairs={{0,3},{1,2},{2,1},{3,0},{4,7},{5,6},{6,5},{7,4},{8,11},{9,10},{10,... | collective-permute-start | bytes 12296 | tf_op jit(solution)/shard_map/ppermute | solution.py:235
  40.8 1.6 %collective-permute-done.5.refs_3_ = f32[8,128]{1,0:T(8,128)S(1)} collective-permute-done((f32[8,128]{1,0:T(8,128)S(1)}, f32[8,128]{1,0:T(8,128)S(1)}, u32[]{:S(2)}, u32[]{:S(2)}) %collective-permute-start.5) | collective-permute-done | bytes 4128 | tf_op jit(solution)/shard_map/ppermute | solution.py:235
  42.4 1.0 %collective-permute-start.12 = (bf16[64,2048]{1,0:T(8,128)(2,1)S(1)}, bf16[64,2048]{1,0:T(8,128)(2,1)S(1)}, u32[]{:S(2)}, u32[]{:S(2)}) collective-permute-start(bf16[64,2048]{1,0:T(8,128)(2,1)S(1)} %get-tuple-element.55), channel_id=1, source_target_pairs={{0,1},{1,0},{2,3},{3,2},{4,5},{5,4},{6,7},{7,6},{8,9},{9,8},{10,11... | collective-permute-start | bytes 786440 | tf_op jit(solution)/shard_map/ppermute | solution.py:235
  43.5 0.0 collective-permute-done.refs_1_
  43.5 2.5 %collective-permute-start.13 = (bf16[64,2048]{1,0:T(8,128)(2,1)S(1)}, bf16[64,2048]{1,0:T(8,128)(2,1)S(1)}, u32[]{:S(2)}, u32[]{:S(2)}) collective-permute-start(bf16[64,2048]{1,0:T(8,128)(2,1)S(1)} %get-tuple-element.56), channel_id=1, source_target_pairs={{0,2},{1,3},{2,0},{3,1},{4,6},{5,7},{6,4},{7,5},{8,10},{9,11},{10,... | collective-permute-start | bytes 786440 | tf_op jit(solution)/shard_map/ppermute | solution.py:235
  45.9 0.0 collective-permute-start.14
  46.0 6.5 %base_product.1.base_ref = f32[256,512]{1,0:T(8,128)S(1)} custom-call(bf16[256,8192]{1,0:T(8,128)(2,1)} %hidden_ref.3, bf16[8192,512]{1,0:T(8,128)(2,1)} %weight_ref.1), custom_call_target="tpu_custom_call" | custom-call | tf_op jit(solution)/shard_map/base_product/pallas_call | solution.py:220
  52.4 0.1 shard_map.64
  52.6 0.5 shard_map.65.refs_0_
  53.1 1.1 %collective-permute-start.19 = (bf16[256,512]{1,0:T(8,128)(2,1)S(1)}, bf16[256,512]{1,0:T(8,128)(2,1)S(1)}, u32[]{:S(2)}, u32[]{:S(2)}) collective-permute-start(bf16[256,512]{1,0:T(8,128)(2,1)S(1)} %copy-done), channel_id=1, source_target_pairs={{0,6},{1,7},{2,4},{3,5},{4,2},{5,3},{6,0},{7,1},{8,14},{9,15},{10,... | collective-permute-start | bytes 786440 | tf_op jit(solution)/shard_map/ppermute | solution.py:235
  54.2 0.0 collective-permute-done.12.refs_1_
  54.2 1.6 %collective-permute-start.7 = (f32[128,128]{1,0:T(8,128)S(1)}, f32[128,128]{1,0:T(8,128)S(1)}, u32[]{:S(2)}, u32[]{:S(2)}) collective-permute-start(f32[128,128]{1,0:T(8,128)S(1)} %shard_map.65.refs_0_), channel_id=1, source_target_pairs={{0,16},{8,24},{16,0},{24,8},{1,17},{9,25},{17,1},{25,9},{2,18},{10... | collective-permute-start | bytes 196616 | tf_op jit(solution)/shard_map/ppermute | solution.py:235
  55.8 5.6 %collective-permute-done.14.refs_3_ = bf16[64,2048]{1,0:T(8,128)(2,1)S(1)} collective-permute-done((bf16[64,2048]{1,0:T(8,128)(2,1)S(1)}, bf16[64,2048]{1,0:T(8,128)(2,1)S(1)}, u32[]{:S(2)}, u32[]{:S(2)}) %collective-permute-start.14) | collective-permute-done | bytes 262176 | tf_op jit(solution)/shard_map/ppermute | solution.py:235
  61.5 0.0 collective-permute-start.8
  61.5 0.0 collective-permute-done.15.refs_5_
  61.5 0.5 shard_map.70.refs_0_
  62.0 1.7 %collective-permute-start.16 = (f32[128,128]{1,0:T(8,128)S(1)}, f32[128,128]{1,0:T(8,128)S(1)}, u32[]{:S(2)}, u32[]{:S(2)}) collective-permute-start(f32[128,128]{1,0:T(8,128)S(1)} %shard_map.70.refs_0_), channel_id=1, source_target_pairs={{0,8},{8,0},{16,24},{24,16},{1,9},{9,1},{17,25},{25,17},{2,10},{10... | collective-permute-start | bytes 196616 | tf_op jit(solution)/shard_map/ppermute | solution.py:235
  63.7 0.0 collective-permute-done.6.refs_1_
  63.7 0.5 collective-permute-start.17
  64.2 0.9 %collective-permute-start.18 = (f32[128,128]{1,0:T(8,128)S(1)}, f32[128,128]{1,0:T(8,128)S(1)}, u32[]{:S(2)}, u32[]{:S(2)}) collective-permute-start(f32[128,128]{1,0:T(8,128)S(1)} %shard_map.70.refs_0_), channel_id=1, source_target_pairs={{0,24},{8,16},{16,8},{24,0},{1,25},{9,17},{17,9},{25,1},{2,26},{10... | collective-permute-start | bytes 196616 | tf_op jit(solution)/shard_map/ppermute | solution.py:235
  65.1 0.7 collective-permute-done.8.refs_3_
  65.8 0.1 shard_map.66.placed_ref
  65.9 0.2 shard_map.67
  66.1 0.1 collective-permute-start.9
  66.2 0.2 shard_map.68
  66.4 4.0 %collective-permute-start.10 = (bf16[64,512]{1,0:T(8,128)(2,1)S(1)}, bf16[64,512]{1,0:T(8,128)(2,1)S(1)}, u32[]{:S(2)}, u32[]{:S(2)}) collective-permute-start(bf16[64,512]{1,0:T(8,128)(2,1)S(1)} %get-tuple-element.53), channel_id=1, source_target_pairs={{0,2},{1,3},{2,0},{3,1},{4,6},{5,7},{6,4},{7,5},{8,10},{9,11},{10,... | collective-permute-start | bytes 196616 | tf_op jit(solution)/shard_map/ppermute | solution.py:235
  70.3 1.6 %collective-permute-start.11 = (bf16[64,512]{1,0:T(8,128)(2,1)S(1)}, bf16[64,512]{1,0:T(8,128)(2,1)S(1)}, u32[]{:S(2)}, u32[]{:S(2)}) collective-permute-start(bf16[64,512]{1,0:T(8,128)(2,1)S(1)} %shard_map.68), channel_id=1, source_target_pairs={{0,3},{1,2},{2,1},{3,0},{4,7},{5,6},{6,5},{7,4},{8,11},{9,10},{10,... | collective-permute-start | bytes 196616 | tf_op jit(solution)/shard_map/ppermute | solution.py:235
  72.0 0.1 shard_map.71.placed_ref
  72.1 0.2 shard_map.72
  72.3 0.1 collective-permute-start.20
  72.4 1.9 %collective-permute-start.21 = (bf16[64,512]{1,0:T(8,128)(2,1)S(1)}, bf16[64,512]{1,0:T(8,128)(2,1)S(1)}, u32[]{:S(2)}, u32[]{:S(2)}) collective-permute-start(bf16[64,512]{1,0:T(8,128)(2,1)S(1)} %get-tuple-element.62), channel_id=1, source_target_pairs={{0,2},{1,3},{2,0},{3,1},{4,6},{5,7},{6,4},{7,5},{8,10},{9,11},{10,... | collective-permute-start | bytes 196616 | tf_op jit(solution)/shard_map/ppermute | solution.py:235
  74.2 0.2 shard_map.73
  74.4 1.7 %collective-permute-start.22 = (bf16[64,512]{1,0:T(8,128)(2,1)S(1)}, bf16[64,512]{1,0:T(8,128)(2,1)S(1)}, u32[]{:S(2)}, u32[]{:S(2)}) collective-permute-start(bf16[64,512]{1,0:T(8,128)(2,1)S(1)} %shard_map.73), channel_id=1, source_target_pairs={{0,3},{1,2},{2,1},{3,0},{4,7},{5,6},{6,5},{7,4},{8,11},{9,10},{10,... | collective-permute-start | bytes 196616 | tf_op jit(solution)/shard_map/ppermute | solution.py:235
  76.1 0.2 shard_map.69.base_ref
  76.3 0.3 collective-permute-done.20.refs_1_
  76.6 0.3 collective-permute-done.21.refs_2_
  77.0 2.7 %collective-permute-done.22.refs_3_ = bf16[64,512]{1,0:T(8,128)(2,1)S(1)} collective-permute-done((bf16[64,512]{1,0:T(8,128)(2,1)S(1)}, bf16[64,512]{1,0:T(8,128)(2,1)S(1)}, u32[]{:S(2)}, u32[]{:S(2)}) %collective-permute-start.22) | collective-permute-done | bytes 65568 | tf_op jit(solution)/shard_map/ppermute | solution.py:235
  79.6 0.9 %shard_map.74 = bf16[256,512]{1,0:T(8,128)(2,1)} custom-call(bf16[256,256]{1,0:T(8,128)(2,1)S(1)} %get-tuple-element.34.spread_ref, f32[256,512]{1,0:T(8,128)S(1)} %shard_map.69.base_ref, bf16[64,512]{1,0:T(8,128)(2,1)S(1)} %get-tuple-element.60.refs_0_, bf16[64,512]{1,0:T(8,128)(2,1)S(1)} %collective-permute-done.20.refs_1_, ...), custom_call_target="tpu_custom_call" | custom-call | tf_op jit(solution)/shard_map/pallas_call | solution.py:201
  (15 shorter events, 0.0 us)
Async XLA Ops:
  0.0 61.5 %collective-permute-start.15 = (bf16[2048,256]{1,0:T(8,128)(2,1)}, bf16[2048,256]{1,0:T(8,128)(2,1)S(1)}, u32[]{:S(2)}, u32[]{:S(2)}) collective-permute-start(bf16[2048,256]{1,0:T(8,128)(2,1)} %refs_5_.1), channel_id=1, source_target_pairs={{0,6},{1,7},{2,4},{3,5},{4,2},{5,3},{6,0},{7,1},{8,14},{9,15},{10,... | collective-permute-start | bytes 3145736 | tf_op jit(solution)/shard_map/ppermute | solution.py:235
  0.5 52.1 %copy-start.1 = (bf16[2048,256]{1,0:T(8,128)(2,1)S(1)}, bf16[2048,256]{1,0:T(8,128)(2,1)}, u32[]{:S(2)}) copy-start(bf16[2048,256]{1,0:T(8,128)(2,1)} %refs_5_.1) | copy-start | bytes 3145732
  2.6 50.5 %copy-start = (bf16[256,512]{1,0:T(8,128)(2,1)S(1)}, bf16[256,512]{1,0:T(8,128)(2,1)}, u32[]{:S(2)}) copy-start(bf16[256,512]{1,0:T(8,128)(2,1)} %up_ref.3) | copy-start | bytes 786436
  2.6 40.9 %collective-permute-start = (bf16[64,2048]{1,0:T(8,128)(2,1)S(1)}, bf16[64,2048]{1,0:T(8,128)(2,1)S(1)}, u32[]{:S(2)}, u32[]{:S(2)}) collective-permute-start(bf16[64,2048]{1,0:T(8,128)(2,1)S(1)} %get-tuple-element.37), channel_id=1, source_target_pairs={{0,1},{1,0},{2,3},{3,2},{4,5},{5,4},{6,7},{7,6},{8,9},{9,8},{10,11... | collective-permute-start | bytes 786440 | tf_op jit(solution)/shard_map/ppermute | solution.py:235
  4.1 41.8 %collective-permute-start.1 = (bf16[64,2048]{1,0:T(8,128)(2,1)S(1)}, bf16[64,2048]{1,0:T(8,128)(2,1)S(1)}, u32[]{:S(2)}, u32[]{:S(2)}) collective-permute-start(bf16[64,2048]{1,0:T(8,128)(2,1)S(1)} %get-tuple-element.38), channel_id=1, source_target_pairs={{0,2},{1,3},{2,0},{3,1},{4,6},{5,7},{6,4},{7,5},{8,10},{9,11},{10,... | collective-permute-start | bytes 786440 | tf_op jit(solution)/shard_map/ppermute | solution.py:235
  5.5 47.1 %collective-permute-start.2 = (bf16[64,2048]{1,0:T(8,128)(2,1)S(1)}, bf16[64,2048]{1,0:T(8,128)(2,1)S(1)}, u32[]{:S(2)}, u32[]{:S(2)}) collective-permute-start(bf16[64,2048]{1,0:T(8,128)(2,1)S(1)} %get-tuple-element.39), channel_id=1, source_target_pairs={{0,3},{1,2},{2,1},{3,0},{4,7},{5,6},{6,5},{7,4},{8,11},{9,10},{10,... | collective-permute-start | bytes 786440 | tf_op jit(solution)/shard_map/ppermute | solution.py:235
  6.1 4.4 %collective-permute-start.3 = (f32[8,128]{1,0:T(8,128)S(1)}, f32[8,128]{1,0:T(8,128)S(1)}, u32[]{:S(2)}, u32[]{:S(2)}) collective-permute-start(f32[8,128]{1,0:T(8,128)S(1)} %get-tuple-element.46), channel_id=1, source_target_pairs={{0,1},{1,0},{2,3},{3,2},{4,5},{5,4},{6,7},{7,6},{8,9},{9,8},{10,11... | collective-permute-start | bytes 12296 | tf_op jit(solution)/shard_map/ppermute | solution.py:235
  10.5 27.0 %collective-permute-start.4 = (f32[8,128]{1,0:T(8,128)S(1)}, f32[8,128]{1,0:T(8,128)S(1)}, u32[]{:S(2)}, u32[]{:S(2)}) collective-permute-start(f32[8,128]{1,0:T(8,128)S(1)} %get-tuple-element.47), channel_id=1, source_target_pairs={{0,2},{1,3},{2,0},{3,1},{4,6},{5,7},{6,4},{7,5},{8,10},{9,11},{10,... | collective-permute-start | bytes 12296 | tf_op jit(solution)/shard_map/ppermute | solution.py:235
  37.5 5.0 %collective-permute-start.5 = (f32[8,128]{1,0:T(8,128)S(1)}, f32[8,128]{1,0:T(8,128)S(1)}, u32[]{:S(2)}, u32[]{:S(2)}) collective-permute-start(f32[8,128]{1,0:T(8,128)S(1)} %get-tuple-element.48), channel_id=1, source_target_pairs={{0,3},{1,2},{2,1},{3,0},{4,7},{5,6},{6,5},{7,4},{8,11},{9,10},{10,... | collective-permute-start | bytes 12296 | tf_op jit(solution)/shard_map/ppermute | solution.py:235
  42.4 11.8 %collective-permute-start.12 = (bf16[64,2048]{1,0:T(8,128)(2,1)S(1)}, bf16[64,2048]{1,0:T(8,128)(2,1)S(1)}, u32[]{:S(2)}, u32[]{:S(2)}) collective-permute-start(bf16[64,2048]{1,0:T(8,128)(2,1)S(1)} %get-tuple-element.55), channel_id=1, source_target_pairs={{0,1},{1,0},{2,3},{3,2},{4,5},{5,4},{6,7},{7,6},{8,9},{9,8},{10,11... | collective-permute-start | bytes 786440 | tf_op jit(solution)/shard_map/ppermute | solution.py:235
  43.5 10.8 %collective-permute-start.13 = (bf16[64,2048]{1,0:T(8,128)(2,1)S(1)}, bf16[64,2048]{1,0:T(8,128)(2,1)S(1)}, u32[]{:S(2)}, u32[]{:S(2)}) collective-permute-start(bf16[64,2048]{1,0:T(8,128)(2,1)S(1)} %get-tuple-element.56), channel_id=1, source_target_pairs={{0,2},{1,3},{2,0},{3,1},{4,6},{5,7},{6,4},{7,5},{8,10},{9,11},{10,... | collective-permute-start | bytes 786440 | tf_op jit(solution)/shard_map/ppermute | solution.py:235
  45.9 15.5 %collective-permute-start.14 = (bf16[64,2048]{1,0:T(8,128)(2,1)S(1)}, bf16[64,2048]{1,0:T(8,128)(2,1)S(1)}, u32[]{:S(2)}, u32[]{:S(2)}) collective-permute-start(bf16[64,2048]{1,0:T(8,128)(2,1)S(1)} %get-tuple-element.57), channel_id=1, source_target_pairs={{0,3},{1,2},{2,1},{3,0},{4,7},{5,6},{6,5},{7,4},{8,11},{9,10},{10,... | collective-permute-start | bytes 786440 | tf_op jit(solution)/shard_map/ppermute | solution.py:235
  53.1 19.0 %collective-permute-start.19 = (bf16[256,512]{1,0:T(8,128)(2,1)S(1)}, bf16[256,512]{1,0:T(8,128)(2,1)S(1)}, u32[]{:S(2)}, u32[]{:S(2)}) collective-permute-start(bf16[256,512]{1,0:T(8,128)(2,1)S(1)} %copy-done), channel_id=1, source_target_pairs={{0,6},{1,7},{2,4},{3,5},{4,2},{5,3},{6,0},{7,1},{8,14},{9,15},{10,... | collective-permute-start | bytes 786440 | tf_op jit(solution)/shard_map/ppermute | solution.py:235
  54.2 9.5 %collective-permute-start.6 = (f32[128,128]{1,0:T(8,128)S(1)}, f32[128,128]{1,0:T(8,128)S(1)}, u32[]{:S(2)}, u32[]{:S(2)}) collective-permute-start(f32[128,128]{1,0:T(8,128)S(1)} %shard_map.65.refs_0_), channel_id=1, source_target_pairs={{0,8},{8,0},{16,24},{24,16},{1,9},{9,1},{17,25},{25,17},{2,10},{10... | collective-permute-start | bytes 196616 | tf_op jit(solution)/shard_map/ppermute | solution.py:235
  54.2 10.0 %collective-permute-start.7 = (f32[128,128]{1,0:T(8,128)S(1)}, f32[128,128]{1,0:T(8,128)S(1)}, u32[]{:S(2)}, u32[]{:S(2)}) collective-permute-start(f32[128,128]{1,0:T(8,128)S(1)} %shard_map.65.refs_0_), channel_id=1, source_target_pairs={{0,16},{8,24},{16,0},{24,8},{1,17},{9,25},{17,1},{25,9},{2,18},{10... | collective-permute-start | bytes 196616 | tf_op jit(solution)/shard_map/ppermute | solution.py:235
  61.5 4.3 %collective-permute-start.8 = (f32[128,128]{1,0:T(8,128)S(1)}, f32[128,128]{1,0:T(8,128)S(1)}, u32[]{:S(2)}, u32[]{:S(2)}) collective-permute-start(f32[128,128]{1,0:T(8,128)S(1)} %shard_map.65.refs_0_), channel_id=1, source_target_pairs={{0,24},{8,16},{16,8},{24,0},{1,25},{9,17},{17,9},{25,1},{2,26},{10... | collective-permute-start | bytes 196616 | tf_op jit(solution)/shard_map/ppermute | solution.py:235
  62.0 4.4 %collective-permute-start.16 = (f32[128,128]{1,0:T(8,128)S(1)}, f32[128,128]{1,0:T(8,128)S(1)}, u32[]{:S(2)}, u32[]{:S(2)}) collective-permute-start(f32[128,128]{1,0:T(8,128)S(1)} %shard_map.70.refs_0_), channel_id=1, source_target_pairs={{0,8},{8,0},{16,24},{24,16},{1,9},{9,1},{17,25},{25,17},{2,10},{10... | collective-permute-start | bytes 196616 | tf_op jit(solution)/shard_map/ppermute | solution.py:235
  63.7 6.7 %collective-permute-start.17 = (f32[128,128]{1,0:T(8,128)S(1)}, f32[128,128]{1,0:T(8,128)S(1)}, u32[]{:S(2)}, u32[]{:S(2)}) collective-permute-start(f32[128,128]{1,0:T(8,128)S(1)} %shard_map.70.refs_0_), channel_id=1, source_target_pairs={{0,16},{8,24},{16,0},{24,8},{1,17},{9,25},{17,1},{25,9},{2,18},{10... | collective-permute-start | bytes 196616 | tf_op jit(solution)/shard_map/ppermute | solution.py:235
  64.2 7.8 %collective-permute-start.18 = (f32[128,128]{1,0:T(8,128)S(1)}, f32[128,128]{1,0:T(8,128)S(1)}, u32[]{:S(2)}, u32[]{:S(2)}) collective-permute-start(f32[128,128]{1,0:T(8,128)S(1)} %shard_map.70.refs_0_), channel_id=1, source_target_pairs={{0,24},{8,16},{16,8},{24,0},{1,25},{9,17},{17,9},{25,1},{2,26},{10... | collective-permute-start | bytes 196616 | tf_op jit(solution)/shard_map/ppermute | solution.py:235
  66.1 8.3 %collective-permute-start.9 = (bf16[64,512]{1,0:T(8,128)(2,1)S(1)}, bf16[64,512]{1,0:T(8,128)(2,1)S(1)}, u32[]{:S(2)}, u32[]{:S(2)}) collective-permute-start(bf16[64,512]{1,0:T(8,128)(2,1)S(1)} %get-tuple-element.52), channel_id=1, source_target_pairs={{0,1},{1,0},{2,3},{3,2},{4,5},{5,4},{6,7},{7,6},{8,9},{9,8},{10,11... | collective-permute-start | bytes 196616 | tf_op jit(solution)/shard_map/ppermute | solution.py:235
  66.4 9.7 %collective-permute-start.10 = (bf16[64,512]{1,0:T(8,128)(2,1)S(1)}, bf16[64,512]{1,0:T(8,128)(2,1)S(1)}, u32[]{:S(2)}, u32[]{:S(2)}) collective-permute-start(bf16[64,512]{1,0:T(8,128)(2,1)S(1)} %get-tuple-element.53), channel_id=1, source_target_pairs={{0,2},{1,3},{2,0},{3,1},{4,6},{5,7},{6,4},{7,5},{8,10},{9,11},{10,... | collective-permute-start | bytes 196616 | tf_op jit(solution)/shard_map/ppermute | solution.py:235
  70.3 5.8 %collective-permute-start.11 = (bf16[64,512]{1,0:T(8,128)(2,1)S(1)}, bf16[64,512]{1,0:T(8,128)(2,1)S(1)}, u32[]{:S(2)}, u32[]{:S(2)}) collective-permute-start(bf16[64,512]{1,0:T(8,128)(2,1)S(1)} %shard_map.68), channel_id=1, source_target_pairs={{0,3},{1,2},{2,1},{3,0},{4,7},{5,6},{6,5},{7,4},{8,11},{9,10},{10,... | collective-permute-start | bytes 196616 | tf_op jit(solution)/shard_map/ppermute | solution.py:235
  72.3 4.3 %collective-permute-start.20 = (bf16[64,512]{1,0:T(8,128)(2,1)S(1)}, bf16[64,512]{1,0:T(8,128)(2,1)S(1)}, u32[]{:S(2)}, u32[]{:S(2)}) collective-permute-start(bf16[64,512]{1,0:T(8,128)(2,1)S(1)} %get-tuple-element.61), channel_id=1, source_target_pairs={{0,1},{1,0},{2,3},{3,2},{4,5},{5,4},{6,7},{7,6},{8,9},{9,8},{10,11... | collective-permute-start | bytes 196616 | tf_op jit(solution)/shard_map/ppermute | solution.py:235
  72.4 4.6 %collective-permute-start.21 = (bf16[64,512]{1,0:T(8,128)(2,1)S(1)}, bf16[64,512]{1,0:T(8,128)(2,1)S(1)}, u32[]{:S(2)}, u32[]{:S(2)}) collective-permute-start(bf16[64,512]{1,0:T(8,128)(2,1)S(1)} %get-tuple-element.62), channel_id=1, source_target_pairs={{0,2},{1,3},{2,0},{3,1},{4,6},{5,7},{6,4},{7,5},{8,10},{9,11},{10,... | collective-permute-start | bytes 196616 | tf_op jit(solution)/shard_map/ppermute | solution.py:235
  74.4 5.2 %collective-permute-start.22 = (bf16[64,512]{1,0:T(8,128)(2,1)S(1)}, bf16[64,512]{1,0:T(8,128)(2,1)S(1)}, u32[]{:S(2)}, u32[]{:S(2)}) collective-permute-start(bf16[64,512]{1,0:T(8,128)(2,1)S(1)} %shard_map.73), channel_id=1, source_target_pairs={{0,3},{1,2},{2,1},{3,0},{4,7},{5,6},{6,5},{7,4},{8,11},{9,10},{10,... | collective-permute-start | bytes 196616 | tf_op jit(solution)/shard_map/ppermute | solution.py:235
